TPU v7x, 32 devices: a whole 2x2x4 slice. The times are simulated.
32 devices in a mesh: groups: 2 (over x), dp: 16 (over z, y, core).
Axes of the slice: x: 2, y: 2, z: 4, core: 2. Of those that a mesh axis runs over, the one named last changes fastest.
Arguments:
- embeddings: bfloat16 [4096, 1024], P(('groups', 'dp')), parts along dimension 0
- cluster_ids: int32 [4096], P(('groups', 'dp')), parts along dimension 0, may hold values from 0 to 511, as said below
- owner: int32 [1024], P('groups'), parts along dimension 0, may hold values from 0 to 15, as said below
Outputs:
- smoothed: bfloat16 [4096, 1024], P(('groups', 'dp')), parts along dimension 0
There are 2 independent parts, one for each index of `groups`. A program takes and returns all parts, laid end to end along the dimension named above; each array names one. Nothing has to cross between parts.
Inputs may be any that keep to these rules, and one draw needn't show every extreme that they name: `owner`: every device number owns exactly 32 clusters. `cluster_ids`: among the rows of one device, at most 16 belong to clusters of one owner, and on every device some owner gets exactly 16 of them.
All inputs are finite; a program needn't handle non-finite values.
Results may differ from a plain program's by a relative error of at most 0.0041.
Values may be sent and summed in bfloat16 or wider, within the bound.
No kernel may reach another device: no remote copies, remote signals or barrier semaphores. Data moves between devices by JAX's collectives and lax.ppermute only.
A program may use at most 64 MiB of HBM per device.

v0:
```python
import jax
import jax.numpy as jnp
from jax import lax
from jax.sharding import PartitionSpec as P

epsilon = 1e-06
sharpness_scale = 0.25


def normalize(rows):
    values = rows.astype(jnp.float32)
    return (values * lax.rsqrt(jnp.sum(values * values, axis=1, keepdims=True) + epsilon)).astype(
        jnp.bfloat16
    )


def kernel_terms(query_unit, query_labels, key_unit, compared_group_ids, key_rows):
    pairwise_similarity = jnp.dot(query_unit, key_unit.T, preferred_element_type=jnp.float32)
    shared_group_filter = (query_labels[:, None] == compared_group_ids[None, :]) & (
        query_labels[:, None] >= 0
    )
    affinity_factor = jnp.where(
        shared_group_filter,
        jnp.exp((pairwise_similarity - 1.0) / sharpness_scale),
        jnp.float32(0.0),
    )
    total = jnp.sum(affinity_factor, axis=1)
    numer = jnp.dot(
        affinity_factor.astype(jnp.bfloat16), key_rows, preferred_element_type=jnp.float32
    )
    return (numer, total)


def finish(numer, total, labels):
    total = jnp.where(labels >= 0, total, jnp.float32(1.0))
    return (numer / total[:, None]).astype(jnp.bfloat16)


def shards(embeddings, cluster_ids, owner):
    peers = lax.axis_size("dp")
    rows_dev, width = embeddings.shape
    slot = 2 * rows_dev // peers
    dest = jnp.take(owner, cluster_ids)
    onehot = (dest[:, None] == jnp.arange(peers, dtype=jnp.int32)[None, :]).astype(jnp.int32)
    rank = jnp.sum(onehot * (jnp.cumsum(onehot, axis=0) - 1), axis=1)
    target = dest * slot + rank
    outgoing = (
        jnp.zeros((peers * slot, width), jnp.bfloat16)
        .at[target]
        .set(embeddings)
        .reshape(peers, slot, width)
    )
    labels = (
        jnp.full((peers * slot,), -1, jnp.int32).at[target].set(cluster_ids).reshape(peers, slot)
    )
    received, got_labels = (
        lax.all_to_all(outgoing, "dp", split_axis=0, concat_axis=0, tiled=True),
        lax.all_to_all(labels, "dp", split_axis=0, concat_axis=0, tiled=True),
    )
    flat_rows = received.reshape(-1, width)
    flat_labels = got_labels.reshape(-1)
    unit = normalize(flat_rows)
    numer, total = kernel_terms(unit, flat_labels, unit, flat_labels, flat_rows)
    result = finish(numer, total, flat_labels).reshape(peers, slot, width)
    back = lax.all_to_all(result, "dp", split_axis=0, concat_axis=0, tiled=True)
    return back.reshape(-1, width)[target]


def solution(mesh):
    placed = (P(("groups", "dp"), None), P(("groups", "dp")), P("groups"))
    return jax.shard_map(
        shards, mesh=mesh, in_specs=placed, out_specs=P(("groups", "dp"), None), check_vma=False
    )
```

profile of v0, /device:TPU:0, one launch (start us, length us, event | category | flops | bytes accessed | tf_op | source)
XLA Modules:
  0.0 57.5 jit_solution(17104505909790052697)
XLA Ops:
  0.0 0.0 copy-start
  0.0 0.7 %compare_select_fusion.1 = s32[128]{0:T(128)S(1)} fusion(s32[128]{0:T(128)} %param.4), kind=kLoop, calls=%fused_computation.24 | loop fusion | flops 384 | bytes 1024 | tf_op jit(solution)/shard_map/jit(_take)/jit(_where)/select_n | solution.py:43
  0.7 0.0 copy-done
  0.7 0.0 copy-start.1
  0.7 1.3 %gather_fusion = s32[128]{0:T(128)S(1)} fusion(s32[512]{0:T(512)S(1)} %copy-done, s32[1024]{0:T(1024)S(1)} %pad_clamp_fusion.1), kind=kCustom, calls=%fused_computation | custom fusion | bytes 1536 | tf_op jit(solution)/shard_map/jit(_take)/gather | solution.py:43
  2.0 0.0 copy-done.1
  2.0 0.1 fusion.9
  2.1 0.2 reduce_window_sum.11
  2.3 0.2 select_reduce_fusion
  2.4 1.0 %scatter_custom_fusion = s32[256]{0:T(256)S(1)} fusion(s32[128]{0:T(128)S(1)} %compare_select_fusion, s32[128]{0:T(128)S(1)} %copy-done.1, s32[]{:T(128)} %constant.13.clone.1), kind=kCustom, calls=%fused_computation.28 | custom fusion | bytes 1028 | tf_op jit(solution)/shard_map/scatter | solution.py:54
  3.4 0.7 %all_to_all.12 = s32[16,1,16]{2,1,0:T(1,128)} reshape(s32[256]{0:T(256)S(1)} %scatter_custom_fusion) | data formatting | bytes 2048 | tf_op jit(solution)/shard_map/all_to_all | solution.py:58
  4.1 7.4 %all-to-all-start = ((s32[16,1,16]{2,1,0:T(1,128)}), s32[16,1,16]{2,1,0:T(1,128)S(1)}, u32[]{:S(2)}, u32[]{:S(2)}) async-start(s32[16,1,16]{2,1,0:T(1,128)} %all_to_all.12), calls=%async_computation | async-start | bytes 16384 | tf_op jit(solution)/shard_map/all_to_all | solution.py:58
  11.5 2.4 %scatter_custom_fusion.1 = bf16[256,1024]{1,0:T(8,128)(2,1)} fusion(s32[128]{0:T(128)S(1)} %compare_select_fusion, bf16[128,1024]{1,0:T(8,128)(2,1)} %param.3, bf16[]{:T(256)} %constant.12.clone.1), kind=kCustom, calls=%fused_computation.14 | custom fusion | bytes 524800 | tf_op jit(solution)/shard_map/scatter | solution.py:50
  13.9 4.0 %all-to-all-done = s32[16,1,16]{2,1,0:T(1,128)S(1)} async-done(((s32[16,1,16]{2,1,0:T(1,128)}), s32[16,1,16]{2,1,0:T(1,128)S(1)}, u32[]{:S(2)}, u32[]{:S(2)}) %all-to-all-start) | async-done | bytes 1056 | tf_op jit(solution)/shard_map/all_to_all | solution.py:58
  17.9 3.6 %all-to-all-start.1 = ((bf16[16,16,1024]{2,1,0:T(8,128)(2,1)}), bf16[16,16,1024]{2,1,0:T(8,128)(2,1)S(1)}, u32[]{:S(2)}, u32[]{:S(2)}) async-start(bf16[16,16,1024]{2,1,0:T(8,128)(2,1)} %bitcast), calls=%async_computation.1 | async-start | bytes 1048576 | tf_op jit(solution)/shard_map/all_to_all | solution.py:57
  21.5 0.5 broadcast.66
  22.0 0.7 %reduce.4 = s32[16,16]{1,0:T(8,128)S(1)} reduce(s32[16,1,16]{2,1,0:T(1,128)S(1)} %all-to-all-done, s32[]{:T(128)} %broadcast.66), dimensions={1}, to_apply=%all_to_all.13.reduce_sub_computation.3 | reduce | bytes 2052 | tf_op jit(solution)/shard_map/all_to_all | solution.py:58
  22.7 0.1 eq.31
  22.8 13.0 %all-to-all-done.1 = bf16[16,16,1024]{2,1,0:T(8,128)(2,1)S(1)} async-done(((bf16[16,16,1024]{2,1,0:T(8,128)(2,1)}), bf16[16,16,1024]{2,1,0:T(8,128)(2,1)S(1)}, u32[]{:S(2)}, u32[]{:S(2)}) %all-to-all-start.1) | async-done | bytes 524320 | tf_op jit(solution)/shard_map/all_to_all | solution.py:57
  35.7 0.2 fusion.4
  35.9 0.2 fusion.5
  36.1 0.4 fusion.12
  36.5 1.1 %fusion = bf16[256,1024]{1,0:T(8,128)(2,1)} fusion(bf16[256,1024]{1,0:T(8,128)(2,1)S(1)} %bitcast.10, f32[256]{0:T(256)S(1)} %broadcast_select_fusion, bf16[256,256]{0,1:T(8,128)(2,1)S(1)} %get-tuple-element.6), kind=kOutput, calls=%fused_computation.7 | convolution fusion | flops 134742016 | bytes 1180672 | tf_op jit(solution)/shard_map/dot_general | solution.py:28
  37.6 4.1 %all-to-all-start.2 = ((bf16[16,16,1024]{2,1,0:T(8,128)(2,1)}), bf16[16,16,1024]{2,1,0:T(8,128)(2,1)S(1)}, u32[]{:S(2)}, u32[]{:S(2)}) async-start(bf16[16,16,1024]{2,1,0:T(8,128)(2,1)} %bitcast.3), calls=%async_computation.2 | async-start | bytes 1048576 | tf_op jit(solution)/shard_map/all_to_all | solution.py:65
  41.7 14.3 %all-to-all-done.2 = bf16[16,16,1024]{2,1,0:T(8,128)(2,1)S(1)} async-done(((bf16[16,16,1024]{2,1,0:T(8,128)(2,1)}), bf16[16,16,1024]{2,1,0:T(8,128)(2,1)S(1)}, u32[]{:S(2)}, u32[]{:S(2)}) %all-to-all-start.2) | async-done | bytes 524320 | tf_op jit(solution)/shard_map/all_to_all | solution.py:65
  55.9 1.6 %gather_fusion.1 = bf16[128,1024]{1,0:T(8,128)(2,1)} fusion(bf16[256,1024]{1,0:T(8,128)(2,1)S(1)} %bitcast.9, s32[1024]{0:T(1024)S(1)} %pad_clamp_fusion), kind=kCustom, calls=%fused_computation.1 | custom fusion | bytes 524800 | tf_op jit(solution)/shard_map/gather | solution.py:66
  (7 shorter events, 0.0 us)
Async XLA Ops:
  0.0 0.7 %copy-start = (s32[512]{0:T(512)S(1)}, s32[512]{0:T(512)}, u32[]{:S(2)}) copy-start(s32[512]{0:T(512)} %param.5) | copy-start | bytes 6148
  0.7 1.3 %copy-start.1 = (s32[128]{0:T(128)S(1)}, s32[128]{0:T(128)}, u32[]{:S(2)}) copy-start(s32[128]{0:T(128)} %param.4) | copy-start | bytes 1540
  4.1 13.8 %all-to-all-start = ((s32[16,1,16]{2,1,0:T(1,128)}), s32[16,1,16]{2,1,0:T(1,128)S(1)}, u32[]{:S(2)}, u32[]{:S(2)}) async-start(s32[16,1,16]{2,1,0:T(1,128)} %all_to_all.12), calls=%async_computation | async-start | bytes 16384 | tf_op jit(solution)/shard_map/all_to_all | solution.py:58
  17.9 17.8 %all-to-all-start.1 = ((bf16[16,16,1024]{2,1,0:T(8,128)(2,1)}), bf16[16,16,1024]{2,1,0:T(8,128)(2,1)S(1)}, u32[]{:S(2)}, u32[]{:S(2)}) async-start(bf16[16,16,1024]{2,1,0:T(8,128)(2,1)} %bitcast), calls=%async_computation.1 | async-start | bytes 1048576 | tf_op jit(solution)/shard_map/all_to_all | solution.py:57
  37.6 18.4 %all-to-all-start.2 = ((bf16[16,16,1024]{2,1,0:T(8,128)(2,1)}), bf16[16,16,1024]{2,1,0:T(8,128)(2,1)S(1)}, u32[]{:S(2)}, u32[]{:S(2)}) async-start(bf16[16,16,1024]{2,1,0:T(8,128)(2,1)} %bitcast.3), calls=%async_computation.2 | async-start | bytes 1048576 | tf_op jit(solution)/shard_map/all_to_all | solution.py:65
where the time goes:
time: 57.9 us; the launch traced here: 57.5 us
  waiting for transfers between devices  31.2 us (54%)
  starting transfers between devices  15.1 us (26%)
  local copies, waits for them, and re-layouts  7.47 us (13%)
  other arithmetic  2.15 us (4%)
  matrix products  1.49 us (3%)
    all_to_all x1, waiting for transfers between devices, shards(): back = lax.all_to_all(result, 'dp', split_axis=0, concat_axis=0, tiled=True)  14.3 us
    all_to_all x1, waiting for transfers between devices, shards(): lax.all_to_all(outgoing, 'dp', split_axis=0, concat_axis=0, tiled=True)  13 us
    all_to_all x1, starting transfers between devices, shards(): lax.all_to_all(labels, 'dp', split_axis=0, concat_axis=0, tiled=True)  7.41 us
    all_to_all x1, starting transfers between devices, shards(): back = lax.all_to_all(result, 'dp', split_axis=0, concat_axis=0, tiled=True)  4.09 us
    all_to_all x1, waiting for transfers between devices, shards(): lax.all_to_all(labels, 'dp', split_axis=0, concat_axis=0, tiled=True)  3.99 us
    all_to_all x1, starting transfers between devices, shards(): lax.all_to_all(outgoing, 'dp', split_axis=0, concat_axis=0, tiled=True)  3.57 us
    scatter x1, local copies, waits for them, and re-layouts, shards(): outgoing = jnp.zeros((peers * slot, width), jnp.bfloat16).at[target].set(...  2.37 us
    gather x1, local copies, waits for them, and re-layouts, shards(): return back.reshape(-1, width)[target]  1.56 us
  transfers between devices with their start and end apart: 3, of which 3 were waited for; matrix products, arithmetic and copies ran while one was open for 6% of the time, Pallas kernels for 0%

commit v1 on v0

--- a/solution.py
+++ b/solution.py
@@ -1,10 +1,14 @@
 import jax
 import jax.numpy as jnp
 from jax import lax
+from jax.experimental import pallas as pl
+from jax.experimental.pallas import tpu as pltpu
 from jax.sharding import PartitionSpec as P
+
 
 epsilon = 1e-06
 sharpness_scale = 0.25
+pad = 8
 
 
 def normalize(rows):
@@ -36,7 +40,7 @@
     return (numer / total[:, None]).astype(jnp.bfloat16)
 
 
-def shards(embeddings, cluster_ids, owner):
+def exchange(embeddings, cluster_ids, owner):
     peers = lax.axis_size("dp")
     rows_dev, width = embeddings.shape
     slot = 2 * rows_dev // peers
@@ -66,6 +70,176 @@
     return back.reshape(-1, width)[target]
 
 
+LAYERS, COLUMNS, CORES = 4, 2, 2
+NEXT = (1, 3, 0, 2)
+BACK = (2, 0, 3, 1)
+STAY = (0, 1, 2, 3)
+
+
+def moves(layers, column, core):
+    return [
+        (
+            (z * COLUMNS + y) * CORES + c,
+            (layers[z] * COLUMNS + (y ^ column)) * CORES + (c ^ core),
+        )
+        for z in range(LAYERS)
+        for y in range(COLUMNS)
+        for c in range(CORES)
+    ]
+
+
+def store_row(out_ref, n, row):
+    high = row.astype(jnp.bfloat16)
+    rest = row - high.astype(jnp.float32)
+    middle = rest.astype(jnp.bfloat16)
+    low = (rest - middle.astype(jnp.float32)).astype(jnp.bfloat16)
+    out_ref[n:, :] = jnp.zeros((pad, out_ref.shape[1]), jnp.bfloat16)
+    out_ref[n:, :n] = high
+    out_ref[n:, n : 2 * n] = middle
+    out_ref[n:, 2 * n : 3 * n] = low
+
+
+def load_row(ref, n):
+    parts = ref[n:, : 3 * n].astype(jnp.float32)
+    return parts[:1, :n] + parts[:1, n : 2 * n] + parts[:1, 2 * n : 3 * n]
+
+
+def as_column(row):
+    n = row.shape[1]
+    return jnp.transpose(jnp.broadcast_to(row, (n, n)))[:, :1]
+
+
+def as_rows(column):
+    n = column.shape[0]
+    return jnp.transpose(jnp.broadcast_to(column, (n, n)))[:pad, :]
+
+
+def cat(values, axis=0):
+    return jnp.concatenate(values, axis=axis)
+
+
+def partial_sums(units, ids, key_units, key_ids, key_rows):
+    gram = lax.dot_general(
+        units, key_units, (((1,), (1,)), ((), ())), preferred_element_type=jnp.float32
+    )
+    weight = jnp.where(ids == key_ids, jnp.exp((gram - 1.0) / sharpness_scale), 0.0)
+    total = jnp.sum(weight, axis=1, keepdims=True)
+    numer = jnp.dot(weight.astype(jnp.bfloat16), key_rows, preferred_element_type=jnp.float32)
+    return numer, total
+
+
+def pair_ids(ref):
+    values = ref[...].astype(jnp.float32)
+    return [values[:1], values[1:2]]
+
+
+def early_body(
+    own, own2, col, col2, ring, ring2, own_ids, col_ids, ring_ids, unit, sums, totals, back
+):
+    n = own.shape[0]
+    rows = [ref[...] for ref in (own, own2, col, col2, ring, ring2)]
+    ids = pair_ids(own_ids) + pair_ids(col_ids) + pair_ids(ring_ids)
+    units = [normalize(r) for r in rows]
+    of_own, of_col, of_ring = as_column(ids[0]), as_column(ids[2]), as_column(ids[4])
+    numer, total = partial_sums(
+        cat([units[0], units[4]]), cat([of_own, of_ring]), cat(units[:4]), cat(ids[:4], 1), cat(rows[:4])
+    )
+    back[:n, :] = numer[n:].astype(jnp.bfloat16)
+    store_row(back, n, as_rows(total[n:]))
+    pair = cat([units[0], units[2]])
+    numer2, total2 = partial_sums(
+        pair, cat([of_own, of_col]), cat(units[4:]), cat(ids[4:], 1), cat(rows[4:])
+    )
+    unit[...] = pair
+    sums[:n, :] = numer[:n] + numer2[:n]
+    sums[n:, :] = numer2[n:]
+    totals[:n, :] = jnp.broadcast_to(total[:n] + total2[:n], (n, n))
+    totals[n:, :] = jnp.broadcast_to(total2[n:], (n, n))
+
+
+def side_body(own_ids, col_ids, far_ids, unit, sums, totals, far, far2, numer, total, side):
+    n = far.shape[0]
+    rows = [far[...], far2[...]]
+    mine = cat([as_column(pair_ids(own_ids)[0]), as_column(pair_ids(col_ids)[0])])
+    part, t = partial_sums(
+        unit[...], mine, cat([normalize(r) for r in rows]), cat(pair_ids(far_ids), 1), cat(rows)
+    )
+    side[:n, :] = (part[n:] + sums[n:, :]).astype(jnp.bfloat16)
+    store_row(side, n, as_rows(t[n:] + totals[n:, :1]))
+    numer[...] = part[:n] + sums[:n, :]
+    total[...] = t[:n] + totals[:n, :]
+
+
+def finish_body(numer, total, back, side, out):
+    n = out.shape[0]
+    t = total[:, :1] + as_column(load_row(back, n)) + as_column(load_row(side, n))
+    sums = numer[...] + back[:n, :].astype(jnp.float32) + side[:n, :].astype(jnp.float32)
+    out[...] = (sums / t).astype(jnp.bfloat16)
+
+
+def call(body, outs, *args, close=True):
+    vmem = pl.BlockSpec(memory_space=pltpu.VMEM)
+    if close:
+        kinds = [pltpu.VMEM(shape, dtype) for shape, dtype in outs]
+    else:
+        kinds = [jax.ShapeDtypeStruct(shape, dtype) for shape, dtype in outs]
+    return pl.pallas_call(
+        body,
+        out_shape=kinds,
+        in_specs=[vmem] * len(args),
+        out_specs=[vmem] * len(outs),
+        compiler_params=pltpu.CompilerParams(vmem_limit_bytes=24 * 2**20),
+    )(*args)
+
+
+def near(*arrays):
+    return [pltpu.with_memory_space_constraint(x, pltpu.VMEM) for x in arrays]
+
+
+def gathered(embeddings, cluster_ids):
+    n, width = embeddings.shape
+
+    def send(rows, layers, column, core):
+        return lax.ppermute(rows, "dp", moves(layers, column, core))
+
+    f32, bf16 = jnp.float32, jnp.bfloat16
+    packet = ((n + pad, width), bf16)
+    own = embeddings
+    ring = send(own, NEXT, 0, 0)
+    col = send(own, STAY, 1, 0)
+    own2 = send(own, STAY, 0, 1)
+    one = cluster_ids[None, :]
+    own_ids = cat([one, send(one, STAY, 0, 1)])
+    ring_ids = send(own_ids, NEXT, 0, 0)
+    col_ids = send(own_ids, STAY, 1, 0)
+    far = send(ring, NEXT, 0, 0)
+    far_ids = send(ring_ids, NEXT, 0, 0)
+    col2 = send(col, STAY, 0, 1)
+    ring2 = send(ring, STAY, 0, 1)
+
+    unit, sums, totals, back = call(
+        early_body,
+        [((2 * n, width), bf16), ((2 * n, width), f32), ((2 * n, n), f32), packet],
+        *near(own, own2, col, col2, ring, ring2, own_ids, col_ids, ring_ids),
+    )
+    back = send(back, BACK, 0, 0)
+    far, sums = lax.optimization_barrier((far, sums))
+    far2 = send(far, STAY, 0, 1)
+    numer, total, side = call(
+        side_body,
+        [((n, width), f32), ((n, n), f32), packet],
+        *near(own_ids, col_ids, far_ids, unit, sums, totals, far, far2),
+    )
+    side = send(side, STAY, 1, 0)
+    return call(finish_body, [((n, width), bf16)], *near(numer, total, back, side), close=False)[0]
+
+
+def shards(embeddings, cluster_ids, owner):
+    if lax.axis_size("dp") == LAYERS * COLUMNS * CORES:
+        return gathered(embeddings, cluster_ids)
+    return exchange(embeddings, cluster_ids, owner)
+
+
 def solution(mesh):
     placed = (P(("groups", "dp"), None), P(("groups", "dp")), P("groups"))
     return jax.shard_map(

time: 57.9 us -> 40 us (0.69)
  waiting for transfers between devices: 31.2 us -> 20.1 us
  local copies, waits for them, and re-layouts: 7.47 us -> 0.95 us
  Pallas kernels: 0 us -> 3.51 us
  other arithmetic: 2.15 us -> 0.01 us
  matrix products: 1.49 us -> 0 us
    all_to_all x3 -> x0, waiting for transfers between devices: 31.2 us -> none  [the longest x1 14.3 us: shards(): back = lax.all_to_all(result, 'dp', split_axis=0, concat_axis=0, tiled=True)]
    ppermute x0 -> x13, waiting for transfers between devices: none -> 20.1 us  [send(): return lax.ppermute(rows, 'dp', moves(layers, column, core))]
    ppermute x0 -> x13, starting transfers between devices: none -> 15.2 us  [send(): return lax.ppermute(rows, 'dp', moves(layers, column, core))]
    all_to_all x3 -> x0, starting transfers between devices: 15.1 us -> none  [the longest x1 7.41 us: shards(): lax.all_to_all(labels, 'dp', split_axis=0, concat_axis=0, tiled=True)]
    pallas_call x0 -> x3, Pallas kernels: none -> 3.51 us  [call(): pl.pallas_call(body, out_shape=kinds, in_specs=[vmem] * len(args), out_sp...]
    scatter x2 -> x0, local copies, waits for them, and re-layouts: 3.35 us -> none  [the longest x1 2.37 us: shards(): outgoing = jnp.zeros((peers * slot, width), jnp.bfloat16).at[target].set(...]
    gather x2 -> x0, local copies, waits for them, and re-layouts: 2.83 us -> none  [the longest x1 1.56 us: shards(): return back.reshape(-1, width)[target]]
    dot_general x2 -> x0, matrix products: 1.49 us -> none  [the longest x1 1.12 us: kernel_terms(): jnp.dot(affinity_factor.astype(jnp.bfloat16), key_rows, preferred_element...]
  transfers between devices with their start and end apart: 3 -> 13, of which waited for: 3 -> 8; matrix products, arithmetic and copies ran while one was open for 6% -> 0% of each run, Pallas kernels for 0% -> 7%
where the time goes in v1:
time: 40 us; the launch traced here: 39.9 us
  waiting for transfers between devices  20.1 us (50%)
  starting transfers between devices  15.2 us (38%)
  Pallas kernels  3.51 us (9%)
  local copies, waits for them, and re-layouts  0.95 us (2%)
    ppermute x13, waiting for transfers between devices, send(): return lax.ppermute(rows, 'dp', moves(layers, column, core))  20.1 us
    ppermute x13, starting transfers between devices, send(): return lax.ppermute(rows, 'dp', moves(layers, column, core))  15.2 us
    pallas_call x3, Pallas kernels, call(): pl.pallas_call(body, out_shape=kinds, in_specs=[vmem] * len(args), out_sp...  3.51 us
    unnamed x4, local copies, waits for them, and re-layouts  0.95 us
  transfers between devices with their start and end apart: 13, of which 8 were waited for; matrix products, arithmetic and copies ran while one was open for 0% of the time, Pallas kernels for 7%

profile of v1, /device:TPU:0, one launch (start us, length us, event | category | flops | bytes accessed | tf_op | source)
XLA Modules:
  0.0 39.9 jit_solution(5066953054885367019)
XLA Ops:
  0.0 0.0 copy-start.1
  0.0 3.1 %collective-permute-start.7 = (bf16[128,1024]{1,0:T(8,128)(2,1)}, bf16[128,1024]{1,0:T(8,128)(2,1)S(1)}, u32[]{:S(2)}, u32[]{:S(2)}) collective-permute-start(bf16[128,1024]{1,0:T(8,128)(2,1)} %own.1), channel_id=1, source_target_pairs={{0,4},{1,5},{2,6},{3,7},{4,12},{5,13},{6,14},{7,15},{8,0},{9,1},{1... | collective-permute-start | bytes 786440 | tf_op jit(solution)/shard_map/ppermute | solution.py:203
  3.1 1.5 %collective-permute-start.5 = (bf16[128,1024]{1,0:T(8,128)(2,1)}, bf16[128,1024]{1,0:T(8,128)(2,1)S(1)}, u32[]{:S(2)}, u32[]{:S(2)}) collective-permute-start(bf16[128,1024]{1,0:T(8,128)(2,1)} %own.1), channel_id=1, source_target_pairs={{0,2},{1,3},{2,0},{3,1},{4,6},{5,7},{6,4},{7,5},{8,10},{9,11},{10,... | collective-permute-start | bytes 786440 | tf_op jit(solution)/shard_map/ppermute | solution.py:203
  4.6 0.0 collective-permute-start.4
  4.6 6.0 %collective-permute-done.7.ring = bf16[128,1024]{1,0:T(8,128)(2,1)S(1)} collective-permute-done((bf16[128,1024]{1,0:T(8,128)(2,1)}, bf16[128,1024]{1,0:T(8,128)(2,1)S(1)}, u32[]{:S(2)}, u32[]{:S(2)}) %collective-permute-start.7) | collective-permute-done | bytes 262176 | tf_op jit(solution)/shard_map/ppermute | solution.py:203
  10.6 0.0 collective-permute-start.8
  10.6 0.4 %collective-permute-done.5.col = bf16[128,1024]{1,0:T(8,128)(2,1)S(1)} collective-permute-done((bf16[128,1024]{1,0:T(8,128)(2,1)}, bf16[128,1024]{1,0:T(8,128)(2,1)S(1)}, u32[]{:S(2)}, u32[]{:S(2)}) %collective-permute-start.5) | collective-permute-done | bytes 262176 | tf_op jit(solution)/shard_map/ppermute | solution.py:203
  11.0 0.1 collective-permute-start.6
  11.1 2.5 %collective-permute-start.9 = (bf16[128,1024]{1,0:T(8,128)(2,1)S(1)}, bf16[128,1024]{1,0:T(8,128)(2,1)S(1)}, u32[]{:S(2)}, u32[]{:S(2)}) collective-permute-start(bf16[128,1024]{1,0:T(8,128)(2,1)S(1)} %collective-permute-done.7.ring), channel_id=1, source_target_pairs={{0,4},{1,5},{2,6},{3,7},{4,12},{5,13},{6,14},{7,15},{8,0},{9,1},{1... | collective-permute-start | bytes 786440 | tf_op jit(solution)/shard_map/ppermute | solution.py:203
  13.6 0.0 copy-done.1
  13.6 0.2 collective-permute-start
  13.9 0.9 %collective-permute-done = s32[1,128]{1,0:T(1,128)S(1)} collective-permute-done((s32[1,128]{1,0:T(1,128)S(1)}, s32[1,128]{1,0:T(1,128)S(1)}, u32[]{:S(2)}, u32[]{:S(2)}) %collective-permute-start) | collective-permute-done | bytes 544 | tf_op jit(solution)/shard_map/ppermute | solution.py:203
  14.8 1.5 %collective-permute-start.1 = (s32[2,128]{1,0:T(2,128)S(1)}, s32[2,128]{1,0:T(2,128)S(1)}, u32[]{:S(2)}, u32[]{:S(2)}) collective-permute-start(s32[2,128]{1,0:T(2,128)S(1)} %pad_add_fusion.own_ids), channel_id=1, source_target_pairs={{0,2},{1,3},{2,0},{3,1},{4,6},{5,7},{6,4},{7,5},{8,10},{9,11},{10,... | collective-permute-start | bytes 3080 | tf_op jit(solution)/shard_map/ppermute | solution.py:203
  16.3 2.1 %collective-permute-done.1.col_ids = s32[2,128]{1,0:T(2,128)S(1)} collective-permute-done((s32[2,128]{1,0:T(2,128)S(1)}, s32[2,128]{1,0:T(2,128)S(1)}, u32[]{:S(2)}, u32[]{:S(2)}) %collective-permute-start.1) | collective-permute-done | bytes 1056 | tf_op jit(solution)/shard_map/ppermute | solution.py:203
  18.4 1.7 %collective-permute-start.2 = (s32[2,128]{1,0:T(2,128)S(1)}, s32[2,128]{1,0:T(2,128)S(1)}, u32[]{:S(2)}, u32[]{:S(2)}) collective-permute-start(s32[2,128]{1,0:T(2,128)S(1)} %pad_add_fusion.own_ids), channel_id=1, source_target_pairs={{0,4},{1,5},{2,6},{3,7},{4,12},{5,13},{6,14},{7,15},{8,0},{9,1},{1... | collective-permute-start | bytes 3080 | tf_op jit(solution)/shard_map/ppermute | solution.py:203
  20.1 2.8 %collective-permute-done.2.ring_ids = s32[2,128]{1,0:T(2,128)S(1)} collective-permute-done((s32[2,128]{1,0:T(2,128)S(1)}, s32[2,128]{1,0:T(2,128)S(1)}, u32[]{:S(2)}, u32[]{:S(2)}) %collective-permute-start.2) | collective-permute-done | bytes 1056 | tf_op jit(solution)/shard_map/ppermute | solution.py:203
  22.8 0.0 collective-permute-done.4.own2
  22.9 0.0 collective-permute-done.8.ring2
  22.9 0.0 collective-permute-done.6.col2
  22.9 0.0 copy-start
  22.9 0.9 %copy-done = bf16[128,1024]{1,0:T(8,128)(2,1)S(1)} copy-done((bf16[128,1024]{1,0:T(8,128)(2,1)S(1)}, bf16[128,1024]{1,0:T(8,128)(2,1)}, u32[]{:S(2)}) %copy-start) | copy-done | bytes 262168
  23.8 1.7 %shard_map.28 = (bf16[256,1024]{1,0:T(8,128)(2,1)S(1)}, f32[256,1024]{1,0:T(8,128)S(1)}, f32[256,128]{1,0:T(8,128)S(1)}, bf16[136,1024]{1,0:T(8,128)(2,1)S(1)}) custom-call(bf16[128,1024]{1,0:T(8,128)(2,1)S(1)} %copy-done, bf16[128,1024]{1,0:T(8,128)(2,1)S(1)} %collective-permute-done.4.own2, bf16[128,1024]{1,0:T(8,128)(2,1)S(1)} %collective-permute-done.5.col, ...), custom_call_target="tpu_custom_call" | custom-call | tf_op jit(solution)/shard_map/pallas_call | solution.py:186
  25.5 0.0 collective-permute-done.9.far
  25.5 0.1 collective-permute-start.10
  25.6 0.8 %collective-permute-start.3 = (s32[2,128]{1,0:T(2,128)S(1)}, s32[2,128]{1,0:T(2,128)S(1)}, u32[]{:S(2)}, u32[]{:S(2)}) collective-permute-start(s32[2,128]{1,0:T(2,128)S(1)} %collective-permute-done.2.ring_ids), channel_id=1, source_target_pairs={{0,4},{1,5},{2,6},{3,7},{4,12},{5,13},{6,14},{7,15},{8,0},{9,1},{1... | collective-permute-start | bytes 3080 | tf_op jit(solution)/shard_map/ppermute | solution.py:203
  26.4 2.1 %collective-permute-start.11 = (bf16[136,1024]{1,0:T(8,128)(2,1)S(1)}, bf16[136,1024]{1,0:T(8,128)(2,1)S(1)}, u32[]{:S(2)}, u32[]{:S(2)}) collective-permute-start(bf16[136,1024]{1,0:T(8,128)(2,1)S(1)} %get-tuple-element.21), channel_id=1, source_target_pairs={{0,8},{1,9},{2,10},{3,11},{4,0},{5,1},{6,2},{7,3},{8,12},{9,13},{1... | collective-permute-start | bytes 835592 | tf_op jit(solution)/shard_map/ppermute | solution.py:203
  28.6 1.5 %collective-permute-done.3.far_ids = s32[2,128]{1,0:T(2,128)S(1)} collective-permute-done((s32[2,128]{1,0:T(2,128)S(1)}, s32[2,128]{1,0:T(2,128)S(1)}, u32[]{:S(2)}, u32[]{:S(2)}) %collective-permute-start.3) | collective-permute-done | bytes 1056 | tf_op jit(solution)/shard_map/ppermute | solution.py:203
  30.1 0.0 collective-permute-done.10.far2
  30.1 0.9 %shard_map.29 = (f32[128,1024]{1,0:T(8,128)S(1)}, f32[128,128]{1,0:T(8,128)S(1)}, bf16[136,1024]{1,0:T(8,128)(2,1)S(1)}) custom-call(s32[2,128]{1,0:T(2,128)S(1)} %pad_add_fusion.own_ids, s32[2,128]{1,0:T(2,128)S(1)} %collective-permute-done.1.col_ids, s32[2,128]{1,0:T(2,128)S(1)} %collective-permute-done.3.far_ids, ...), custom_call_target="tpu_custom_call" | custom-call | tf_op jit(solution)/shard_map/pallas_call | solution.py:186
  31.1 1.6 %collective-permute-start.12 = (bf16[136,1024]{1,0:T(8,128)(2,1)S(1)}, bf16[136,1024]{1,0:T(8,128)(2,1)S(1)}, u32[]{:S(2)}, u32[]{:S(2)}) collective-permute-start(bf16[136,1024]{1,0:T(8,128)(2,1)S(1)} %get-tuple-element.22), channel_id=1, source_target_pairs={{0,2},{1,3},{2,0},{3,1},{4,6},{5,7},{6,4},{7,5},{8,10},{9,11},{10,... | collective-permute-start | bytes 835592 | tf_op jit(solution)/shard_map/ppermute | solution.py:203
  32.6 2.5 %collective-permute-done.11.back = bf16[136,1024]{1,0:T(8,128)(2,1)S(1)} collective-permute-done((bf16[136,1024]{1,0:T(8,128)(2,1)S(1)}, bf16[136,1024]{1,0:T(8,128)(2,1)S(1)}, u32[]{:S(2)}, u32[]{:S(2)}) %collective-permute-start.11) | collective-permute-done | bytes 278560 | tf_op jit(solution)/shard_map/ppermute | solution.py:203
  35.2 3.8 %collective-permute-done.12.side = bf16[136,1024]{1,0:T(8,128)(2,1)S(1)} collective-permute-done((bf16[136,1024]{1,0:T(8,128)(2,1)S(1)}, bf16[136,1024]{1,0:T(8,128)(2,1)S(1)}, u32[]{:S(2)}, u32[]{:S(2)}) %collective-permute-start.12) | collective-permute-done | bytes 278560 | tf_op jit(solution)/shard_map/ppermute | solution.py:203
  39.0 0.9 %shard_map.30 = bf16[128,1024]{1,0:T(8,128)(2,1)} custom-call(f32[128,1024]{1,0:T(8,128)S(1)} %get-tuple-element.19.numer, f32[128,128]{1,0:T(8,128)S(1)} %get-tuple-element.20.total, bf16[136,1024]{1,0:T(8,128)(2,1)S(1)} %collective-permute-done.11.back, bf16[136,1024]{1,0:T(8,128)(2,1)S(1)} %collective-permute-done.12.side), custom_call_target="tpu_custom_call" | custom-call | tf_op jit(solution)/shard_map/pallas_call | solution.py:186
  (1 shorter events, 0.0 us)
Async XLA Ops:
  0.0 13.6 %copy-start.1 = (s32[128]{0:T(128)S(1)}, s32[128]{0:T(128)}, u32[]{:S(2)}) copy-start(s32[128]{0:T(128)} %param.4) | copy-start | bytes 1540
  0.0 10.6 %collective-permute-start.7 = (bf16[128,1024]{1,0:T(8,128)(2,1)}, bf16[128,1024]{1,0:T(8,128)(2,1)S(1)}, u32[]{:S(2)}, u32[]{:S(2)}) collective-permute-start(bf16[128,1024]{1,0:T(8,128)(2,1)} %own.1), channel_id=1, source_target_pairs={{0,4},{1,5},{2,6},{3,7},{4,12},{5,13},{6,14},{7,15},{8,0},{9,1},{1... | collective-permute-start | bytes 786440 | tf_op jit(solution)/shard_map/ppermute | solution.py:203
  3.1 8.0 %collective-permute-start.5 = (bf16[128,1024]{1,0:T(8,128)(2,1)}, bf16[128,1024]{1,0:T(8,128)(2,1)S(1)}, u32[]{:S(2)}, u32[]{:S(2)}) collective-permute-start(bf16[128,1024]{1,0:T(8,128)(2,1)} %own.1), channel_id=1, source_target_pairs={{0,2},{1,3},{2,0},{3,1},{4,6},{5,7},{6,4},{7,5},{8,10},{9,11},{10,... | collective-permute-start | bytes 786440 | tf_op jit(solution)/shard_map/ppermute | solution.py:203
  4.6 18.3 %collective-permute-start.4 = (bf16[128,1024]{1,0:T(8,128)(2,1)}, bf16[128,1024]{1,0:T(8,128)(2,1)S(1)}, u32[]{:S(2)}, u32[]{:S(2)}) collective-permute-start(bf16[128,1024]{1,0:T(8,128)(2,1)} %own.1), channel_id=1, source_target_pairs={{0,1},{1,0},{2,3},{3,2},{4,5},{5,4},{6,7},{7,6},{8,9},{9,8},{10,11... | collective-permute-start | bytes 786440 | tf_op jit(solution)/shard_map/ppermute | solution.py:203
  10.6 12.3 %collective-permute-start.8 = (bf16[128,1024]{1,0:T(8,128)(2,1)S(1)}, bf16[128,1024]{1,0:T(8,128)(2,1)S(1)}, u32[]{:S(2)}, u32[]{:S(2)}) collective-permute-start(bf16[128,1024]{1,0:T(8,128)(2,1)S(1)} %collective-permute-done.7.ring), channel_id=1, source_target_pairs={{0,1},{1,0},{2,3},{3,2},{4,5},{5,4},{6,7},{7,6},{8,9},{9,8},{10,11... | collective-permute-start | bytes 786440 | tf_op jit(solution)/shard_map/ppermute | solution.py:203
  11.0 11.8 %collective-permute-start.6 = (bf16[128,1024]{1,0:T(8,128)(2,1)S(1)}, bf16[128,1024]{1,0:T(8,128)(2,1)S(1)}, u32[]{:S(2)}, u32[]{:S(2)}) collective-permute-start(bf16[128,1024]{1,0:T(8,128)(2,1)S(1)} %collective-permute-done.5.col), channel_id=1, source_target_pairs={{0,1},{1,0},{2,3},{3,2},{4,5},{5,4},{6,7},{7,6},{8,9},{9,8},{10,11... | collective-permute-start | bytes 786440 | tf_op jit(solution)/shard_map/ppermute | solution.py:203
  11.1 14.4 %collective-permute-start.9 = (bf16[128,1024]{1,0:T(8,128)(2,1)S(1)}, bf16[128,1024]{1,0:T(8,128)(2,1)S(1)}, u32[]{:S(2)}, u32[]{:S(2)}) collective-permute-start(bf16[128,1024]{1,0:T(8,128)(2,1)S(1)} %collective-permute-done.7.ring), channel_id=1, source_target_pairs={{0,4},{1,5},{2,6},{3,7},{4,12},{5,13},{6,14},{7,15},{8,0},{9,1},{1... | collective-permute-start | bytes 786440 | tf_op jit(solution)/shard_map/ppermute | solution.py:203
  13.6 1.2 %collective-permute-start = (s32[1,128]{1,0:T(1,128)S(1)}, s32[1,128]{1,0:T(1,128)S(1)}, u32[]{:S(2)}, u32[]{:S(2)}) collective-permute-start(s32[1,128]{1,0:T(1,128)S(1)} %bitcast.1), channel_id=1, source_target_pairs={{0,1},{1,0},{2,3},{3,2},{4,5},{5,4},{6,7},{7,6},{8,9},{9,8},{10,11... | collective-permute-start | bytes 1544 | tf_op jit(solution)/shard_map/ppermute | solution.py:203
  14.8 3.6 %collective-permute-start.1 = (s32[2,128]{1,0:T(2,128)S(1)}, s32[2,128]{1,0:T(2,128)S(1)}, u32[]{:S(2)}, u32[]{:S(2)}) collective-permute-start(s32[2,128]{1,0:T(2,128)S(1)} %pad_add_fusion.own_ids), channel_id=1, source_target_pairs={{0,2},{1,3},{2,0},{3,1},{4,6},{5,7},{6,4},{7,5},{8,10},{9,11},{10,... | collective-permute-start | bytes 3080 | tf_op jit(solution)/shard_map/ppermute | solution.py:203
  18.4 4.5 %collective-permute-start.2 = (s32[2,128]{1,0:T(2,128)S(1)}, s32[2,128]{1,0:T(2,128)S(1)}, u32[]{:S(2)}, u32[]{:S(2)}) collective-permute-start(s32[2,128]{1,0:T(2,128)S(1)} %pad_add_fusion.own_ids), channel_id=1, source_target_pairs={{0,4},{1,5},{2,6},{3,7},{4,12},{5,13},{6,14},{7,15},{8,0},{9,1},{1... | collective-permute-start | bytes 3080 | tf_op jit(solution)/shard_map/ppermute | solution.py:203
  22.9 1.0 %copy-start = (bf16[128,1024]{1,0:T(8,128)(2,1)S(1)}, bf16[128,1024]{1,0:T(8,128)(2,1)}, u32[]{:S(2)}) copy-start(bf16[128,1024]{1,0:T(8,128)(2,1)} %own.1) | copy-start | bytes 786436
  25.5 4.6 %collective-permute-start.10 = (bf16[128,1024]{1,0:T(8,128)(2,1)S(1)}, bf16[128,1024]{1,0:T(8,128)(2,1)S(1)}, u32[]{:S(2)}, u32[]{:S(2)}) collective-permute-start(bf16[128,1024]{1,0:T(8,128)(2,1)S(1)} %collective-permute-done.9.far), channel_id=1, source_target_pairs={{0,1},{1,0},{2,3},{3,2},{4,5},{5,4},{6,7},{7,6},{8,9},{9,8},{10,11... | collective-permute-start | bytes 786440 | tf_op jit(solution)/shard_map/ppermute | solution.py:203
  25.6 4.5 %collective-permute-start.3 = (s32[2,128]{1,0:T(2,128)S(1)}, s32[2,128]{1,0:T(2,128)S(1)}, u32[]{:S(2)}, u32[]{:S(2)}) collective-permute-start(s32[2,128]{1,0:T(2,128)S(1)} %collective-permute-done.2.ring_ids), channel_id=1, source_target_pairs={{0,4},{1,5},{2,6},{3,7},{4,12},{5,13},{6,14},{7,15},{8,0},{9,1},{1... | collective-permute-start | bytes 3080 | tf_op jit(solution)/shard_map/ppermute | solution.py:203
  26.4 8.7 %collective-permute-start.11 = (bf16[136,1024]{1,0:T(8,128)(2,1)S(1)}, bf16[136,1024]{1,0:T(8,128)(2,1)S(1)}, u32[]{:S(2)}, u32[]{:S(2)}) collective-permute-start(bf16[136,1024]{1,0:T(8,128)(2,1)S(1)} %get-tuple-element.21), channel_id=1, source_target_pairs={{0,8},{1,9},{2,10},{3,11},{4,0},{5,1},{6,2},{7,3},{8,12},{9,13},{1... | collective-permute-start | bytes 835592 | tf_op jit(solution)/shard_map/ppermute | solution.py:203
  31.1 7.9 %collective-permute-start.12 = (bf16[136,1024]{1,0:T(8,128)(2,1)S(1)}, bf16[136,1024]{1,0:T(8,128)(2,1)S(1)}, u32[]{:S(2)}, u32[]{:S(2)}) collective-permute-start(bf16[136,1024]{1,0:T(8,128)(2,1)S(1)} %get-tuple-element.22), channel_id=1, source_target_pairs={{0,2},{1,3},{2,0},{3,1},{4,6},{5,7},{6,4},{7,5},{8,10},{9,11},{10,... | collective-permute-start | bytes 835592 | tf_op jit(solution)/shard_map/ppermute | solution.py:203

commit v2 on v0

--- a/solution.py
+++ b/solution.py
@@ -1,10 +1,14 @@
 import jax
 import jax.numpy as jnp
 from jax import lax
+from jax.experimental import pallas as pl
+from jax.experimental.pallas import tpu as pltpu
 from jax.sharding import PartitionSpec as P
+
 
 epsilon = 1e-06
 sharpness_scale = 0.25
+pad = 8
 
 
 def normalize(rows):
@@ -36,7 +40,7 @@
     return (numer / total[:, None]).astype(jnp.bfloat16)
 
 
-def shards(embeddings, cluster_ids, owner):
+def exchange(embeddings, cluster_ids, owner):
     peers = lax.axis_size("dp")
     rows_dev, width = embeddings.shape
     slot = 2 * rows_dev // peers
@@ -66,6 +70,241 @@
     return back.reshape(-1, width)[target]
 
 
+LAYERS, COLUMNS, CORES = 4, 2, 2
+NEXT = (1, 3, 0, 2)
+BACK = (2, 0, 3, 1)
+STAY = (0, 1, 2, 3)
+
+
+def moves(layers, column, core):
+    return [
+        (
+            (z * COLUMNS + y) * CORES + c,
+            (layers[z] * COLUMNS + (y ^ column)) * CORES + (c ^ core),
+        )
+        for z in range(LAYERS)
+        for y in range(COLUMNS)
+        for c in range(CORES)
+    ]
+
+
+def store_row(out_ref, n, at, row):
+    high = row.astype(jnp.bfloat16)
+    rest = row - high.astype(jnp.float32)
+    middle = rest.astype(jnp.bfloat16)
+    low = (rest - middle.astype(jnp.float32)).astype(jnp.bfloat16)
+    out_ref[at:, :] = jnp.zeros((pad, out_ref.shape[1]), jnp.bfloat16)
+    out_ref[at:, :n] = high
+    out_ref[at:, n : 2 * n] = middle
+    out_ref[at:, 2 * n : 3 * n] = low
+
+
+def load_row(ref, n):
+    at = ref.shape[0] - pad
+    parts = ref[at:, : 3 * n].astype(jnp.float32)
+    return parts[:1, :n] + parts[:1, n : 2 * n] + parts[:1, 2 * n : 3 * n]
+
+
+def as_column(row):
+    n = row.shape[1]
+    return jnp.transpose(jnp.broadcast_to(row, (n, n)))[:, :1]
+
+
+def as_rows(column):
+    n = column.shape[0]
+    return jnp.transpose(jnp.broadcast_to(column, (n, n)))[:pad, :]
+
+
+def cat(values, axis=0):
+    return jnp.concatenate(values, axis=axis)
+
+
+def weights(units, ids, key_units, key_ids):
+    gram = lax.dot_general(
+        units, key_units, (((1,), (1,)), ((), ())), preferred_element_type=jnp.float32
+    )
+    weight = jnp.where(ids == key_ids, jnp.exp((gram - 1.0) / sharpness_scale), 0.0)
+    return weight.astype(jnp.bfloat16), jnp.sum(weight, axis=1, keepdims=True)
+
+
+def weighted(weight, rows):
+    return jnp.dot(weight, rows, preferred_element_type=jnp.float32)
+
+
+def join_body(rows, ids, out):
+    n = rows.shape[0]
+    out[:n, :] = rows[...]
+    store_row(out, n, n, jnp.broadcast_to(ids[...].astype(jnp.float32), (pad, n)))
+
+
+def split_body(rows, ids, out, first, second):
+    n = rows.shape[0]
+    half = n // 2
+    row = jnp.broadcast_to(ids[...].astype(jnp.float32), (pad, n))
+    out[:n, :] = rows[...]
+    store_row(out, n, n, row)
+    first[:half, :] = rows[:half, :]
+    store_row(first, n, half, row)
+    second[...] = rows[half:, :]
+
+
+def early_body(own, own2, col, col2, ring, ring2, own_ids, own2_ids, unit, sums, totals, back):
+    n = own.shape[0]
+    blocks = (col, col2, ring, ring2)
+    rows = [own[...], own2[...]] + [ref[:n, :] for ref in blocks]
+    ids = [ref[...].astype(jnp.float32) for ref in (own_ids, own2_ids)]
+    ids += [load_row(ref, n) for ref in blocks]
+    units = [normalize(r) for r in rows]
+    of_own, of_ring = as_column(ids[0]), as_column(ids[4])
+    weight, total = weights(
+        cat([units[0], units[4]]), cat([of_own, of_ring]), cat(units[:4]), cat(ids[:4], 1)
+    )
+    numer = weighted(weight, cat(rows[:4]))
+    back[:n, :] = numer[n:].astype(jnp.bfloat16)
+    store_row(back, n, n, as_rows(total[n:]))
+    weight2, total2 = weights(units[0], of_own, cat(units[4:]), cat(ids[4:], 1))
+    unit[...] = units[0]
+    sums[...] = numer[:n] + weighted(weight2, cat(rows[4:]))
+    totals[...] = jnp.broadcast_to(total[:n] + total2, (n, n))
+
+
+def key_sums(unit, ids, keys):
+    rows = cat([row for row, _ in keys])
+    weight, total = weights(
+        unit[...], as_column(ids[...].astype(jnp.float32)), cat([normalize(row) for row, _ in keys]),
+        cat([row for _, row in keys], 1),
+    )
+    return weighted(weight, rows), total
+
+
+def keys_of(ref, n):
+    return ref[:n, :], load_row(ref, n)
+
+
+def first_of(ref, n):
+    return ref[: n // 2, :], load_row(ref, n)[:, : n // 2]
+
+
+def second_of(ref, first, n):
+    return ref[...], load_row(first, n)[:, n // 2 :]
+
+
+def add_to(sums, totals, new_sums, new_totals, unit, ids, keys):
+    numer, total = key_sums(unit, ids, keys)
+    new_sums[...] = sums[...] + numer
+    new_totals[...] = totals[...] + total
+
+
+def mid_body(unit, ids, sums, totals, side, side2, fa, fa2, new_sums, new_totals):
+    n = unit.shape[0]
+    keys = [keys_of(side, n), keys_of(side2, n), first_of(fa, n), first_of(fa2, n)]
+    add_to(sums, totals, new_sums, new_totals, unit, ids, keys)
+
+
+def late_body(unit, ids, sums, totals, fa, fa2, fb, fb2, sa, sb, new_sums, new_totals):
+    n = unit.shape[0]
+    keys = [second_of(fb, fa, n), second_of(fb2, fa2, n), first_of(sa, n), second_of(sb, sa, n)]
+    add_to(sums, totals, new_sums, new_totals, unit, ids, keys)
+
+
+def finish_body(unit, ids, sums, totals, sa2, sb2, back, out, near_out, sems):
+    n = unit.shape[0]
+    numer, total = key_sums(unit, ids, [first_of(sa2, n), second_of(sb2, sa2, n)])
+    scale = 1.0 / (total + totals[:, :1] + as_column(load_row(back, n)))
+    step = n // 4
+    copies = []
+    for k in range(4):
+        at = slice(k * step, (k + 1) * step)
+        near_out[at, :] = (
+            (numer[at] + sums[at, :] + back[at, :].astype(jnp.float32)) * scale[at]
+        ).astype(jnp.bfloat16)
+        here = pl.ds(k * step, step)
+        copies.append(pltpu.make_async_copy(near_out.at[here], out.at[here], sems.at[k]))
+        copies[-1].start()
+    for copy in copies:
+        copy.wait()
+
+
+def call(body, outs, *args, out_space=pltpu.VMEM, scratch=()):
+    vmem = pl.BlockSpec(memory_space=pltpu.VMEM)
+    kind = pltpu.VMEM if out_space is pltpu.VMEM else jax.ShapeDtypeStruct
+    return pl.pallas_call(
+        body,
+        out_shape=[kind(shape, dtype) for shape, dtype in outs],
+        in_specs=[vmem] * len(args),
+        out_specs=[pl.BlockSpec(memory_space=out_space)] * len(outs),
+        scratch_shapes=scratch,
+        compiler_params=pltpu.CompilerParams(vmem_limit_bytes=24 * 2**20),
+    )(*args)
+
+
+def near(*arrays):
+    return [pltpu.with_memory_space_constraint(x, pltpu.VMEM) for x in arrays]
+
+
+def gathered(embeddings, cluster_ids):
+    n, width = embeddings.shape
+    half = n // 2
+    f32, bf16 = jnp.float32, jnp.bfloat16
+
+    def send(rows, layers, column, core):
+        return lax.ppermute(rows, "dp", moves(layers, column, core))
+
+    def swap(rows):
+        return send(rows, STAY, 0, 1)
+
+    def join(rows, ids):
+        return call(join_body, [packet], *near(rows, ids))[0]
+
+    packet = ((n + pad, width), bf16)
+    own, ids = embeddings, cluster_ids[None, :]
+    ring = send(own, NEXT, 0, 0)
+    ring_ids = send(ids, NEXT, 0, 0)
+    col = send(own, STAY, 1, 0)
+    col_ids = send(ids, STAY, 1, 0)
+    own2 = swap(own)
+    own2_ids = swap(ids)
+    packet1, packet2 = ((half + pad, width), bf16), ((half, width), bf16)
+    ring, ra, rb = call(split_body, [packet, packet1, packet2], *near(ring, ring_ids))
+    fa = send(ra, NEXT, 0, 0)
+    side = send(ring, STAY, 1, 0)
+    ring2 = swap(ring)
+    fb = send(rb, NEXT, 0, 0)
+    col = join(col, col_ids)
+    col2 = swap(col)
+
+    state = [((n, width), f32), ((n, n), f32)]
+    unit, sums, totals, back = call(
+        early_body,
+        [((n, width), bf16)] + state + [packet],
+        *near(own, own2, col, col2, ring, ring2, ids, own2_ids),
+    )
+    fa, sums = lax.optimization_barrier((fa, sums))
+    sa = send(fa, STAY, 1, 0)
+    fa2 = swap(fa)
+    back = send(back, BACK, 0, 0)
+    sb = send(fb, STAY, 1, 0)
+    fb2 = swap(fb)
+    side2 = swap(side)
+    fb, side2 = lax.optimization_barrier((fb, side2))
+    sums, totals = call(mid_body, state, *near(unit, ids, sums, totals, side, side2, fa, fa2))
+    sa, totals = lax.optimization_barrier((sa, totals))
+    sa2 = swap(sa)
+    sb2 = swap(sb)
+    sums, totals = call(late_body, state, *near(unit, ids, sums, totals, fa, fa2, fb, fb2, sa, sb))
+    out = ((n, width), bf16)
+    return call(
+        finish_body, [out], *near(unit, ids, sums, totals, sa2, sb2, back),
+        out_space=pl.ANY, scratch=[pltpu.VMEM(*out), pltpu.SemaphoreType.DMA((4,))],
+    )[0]
+
+
+def shards(embeddings, cluster_ids, owner):
+    if lax.axis_size("dp") == LAYERS * COLUMNS * CORES:
+        return gathered(embeddings, cluster_ids)
+    return exchange(embeddings, cluster_ids, owner)
+
+
 def solution(mesh):
     placed = (P(("groups", "dp"), None), P(("groups", "dp")), P("groups"))
     return jax.shard_map(

time: 57.9 us -> 39.9 us (0.69)
  waiting for transfers between devices: 31.2 us -> 17.5 us
  local copies, waits for them, and re-layouts: 7.47 us -> 0.01 us
  Pallas kernels: 0 us -> 4.46 us
  starting transfers between devices: 15.1 us -> 17.7 us
  other arithmetic: 2.15 us -> 0 us
  matrix products: 1.49 us -> 0 us
    all_to_all x3 -> x0, waiting for transfers between devices: 31.2 us -> none  [the longest x1 14.3 us: shards(): back = lax.all_to_all(result, 'dp', split_axis=0, concat_axis=0, tiled=True)]
    ppermute x0 -> x19, starting transfers between devices: none -> 17.7 us  [send(): return lax.ppermute(rows, 'dp', moves(layers, column, core))]
    ppermute x0 -> x19, waiting for transfers between devices: none -> 17.5 us  [send(): return lax.ppermute(rows, 'dp', moves(layers, column, core))]
    all_to_all x3 -> x0, starting transfers between devices: 15.1 us -> none  [the longest x1 7.41 us: shards(): lax.all_to_all(labels, 'dp', split_axis=0, concat_axis=0, tiled=True)]
    pallas_call x0 -> x6, Pallas kernels: none -> 4.46 us  [call(): pl.pallas_call(body, out_shape=[kind(shape, dtype) for shape, dtype in ou...]
    scatter x2 -> x0, local copies, waits for them, and re-layouts: 3.35 us -> none  [the longest x1 2.37 us: shards(): outgoing = jnp.zeros((peers * slot, width), jnp.bfloat16).at[target].set(...]
    gather x2 -> x0, local copies, waits for them, and re-layouts: 2.83 us -> none  [the longest x1 1.56 us: shards(): return back.reshape(-1, width)[target]]
    dot_general x2 -> x0, matrix products: 1.49 us -> none  [the longest x1 1.12 us: kernel_terms(): jnp.dot(affinity_factor.astype(jnp.bfloat16), key_rows, preferred_element...]
  transfers between devices with their start and end apart: 3 -> 19, of which waited for: 3 -> 7; matrix products, arithmetic and copies ran while one was open for 6% -> 0% of each run, Pallas kernels for 0% -> 8%
where the time goes in v2:
time: 39.9 us; the launch traced here: 39.7 us
  starting transfers between devices  17.7 us (44%)
  waiting for transfers between devices  17.5 us (44%)
  Pallas kernels  4.46 us (11%)
    ppermute x19, starting transfers between devices, send(): return lax.ppermute(rows, 'dp', moves(layers, column, core))  17.7 us
    ppermute x19, waiting for transfers between devices, send(): return lax.ppermute(rows, 'dp', moves(layers, column, core))  17.5 us
    pallas_call x6, Pallas kernels, call(): pl.pallas_call(body, out_shape=[kind(shape, dtype) for shape, dtype in ou...  4.46 us
  transfers between devices with their start and end apart: 19, of which 7 were waited for; matrix products, arithmetic and copies ran while one was open for 0% of the time, Pallas kernels for 8%

profile of v2, /device:TPU:0, one launch (start us, length us, event | category | flops | bytes accessed | tf_op | source)
XLA Modules:
  0.0 39.7 jit_solution(592451119007729500)
XLA Ops:
  0.0 0.0 copy-start
  0.0 3.1 %collective-permute-start.4 = (bf16[128,1024]{1,0:T(8,128)(2,1)}, bf16[128,1024]{1,0:T(8,128)(2,1)S(1)}, u32[]{:S(2)}, u32[]{:S(2)}) collective-permute-start(bf16[128,1024]{1,0:T(8,128)(2,1)} %own.1), channel_id=1, source_target_pairs={{0,4},{1,5},{2,6},{3,7},{4,12},{5,13},{6,14},{7,15},{8,0},{9,1},{1... | collective-permute-start | bytes 786440 | tf_op jit(solution)/shard_map/ppermute | solution.py:251
  3.1 1.5 %collective-permute-start.1 = (bf16[128,1024]{1,0:T(8,128)(2,1)}, bf16[128,1024]{1,0:T(8,128)(2,1)S(1)}, u32[]{:S(2)}, u32[]{:S(2)}) collective-permute-start(bf16[128,1024]{1,0:T(8,128)(2,1)} %own.1), channel_id=1, source_target_pairs={{0,2},{1,3},{2,0},{3,1},{4,6},{5,7},{6,4},{7,5},{8,10},{9,11},{10,... | collective-permute-start | bytes 786440 | tf_op jit(solution)/shard_map/ppermute | solution.py:251
  4.6 2.6 %collective-permute-start.5 = (s32[1,128]{1,0:T(1,128)}, s32[1,128]{1,0:T(1,128)S(1)}, u32[]{:S(2)}, u32[]{:S(2)}) collective-permute-start(s32[1,128]{1,0:T(1,128)} %bitcast.1), channel_id=1, source_target_pairs={{0,4},{1,5},{2,6},{3,7},{4,12},{5,13},{6,14},{7,15},{8,0},{9,1},{1... | collective-permute-start | bytes 1544 | tf_op jit(solution)/shard_map/ppermute | solution.py:251
  7.2 3.6 %collective-permute-done.5.ids = s32[1,128]{1,0:T(1,128)S(1)} collective-permute-done((s32[1,128]{1,0:T(1,128)}, s32[1,128]{1,0:T(1,128)S(1)}, u32[]{:S(2)}, u32[]{:S(2)}) %collective-permute-start.5) | collective-permute-done | bytes 544 | tf_op jit(solution)/shard_map/ppermute | solution.py:251
  10.7 0.0 collective-permute-done.4.rows
  10.8 0.0 copy-start.1
  10.8 1.6 %collective-permute-start.9 = (bf16[136,1024]{1,0:T(8,128)(2,1)S(1)}, bf16[136,1024]{1,0:T(8,128)(2,1)S(1)}, u32[]{:S(2)}, u32[]{:S(2)}) collective-permute-start(bf16[136,1024]{1,0:T(8,128)(2,1)S(1)} %get-tuple-element.22.ring), channel_id=1, source_target_pairs={{0,2},{1,3},{2,0},{3,1},{4,6},{5,7},{6,4},{7,5},{8,10},{9,11},{10,... | collective-permute-start | bytes 835592 | tf_op jit(solution)/shard_map/ppermute | solution.py:251
  12.4 0.0 copy-done
  12.4 0.0 collective-permute-start
  12.4 0.0 copy-done.1
  12.4 0.6 %collective-permute-start.2 = (s32[1,128]{1,0:T(1,128)S(1)}, s32[1,128]{1,0:T(1,128)S(1)}, u32[]{:S(2)}, u32[]{:S(2)}) collective-permute-start(s32[1,128]{1,0:T(1,128)S(1)} %bitcast.2), channel_id=1, source_target_pairs={{0,2},{1,3},{2,0},{3,1},{4,6},{5,7},{6,4},{7,5},{8,10},{9,11},{10,... | collective-permute-start | bytes 1544 | tf_op jit(solution)/shard_map/ppermute | solution.py:251
  13.0 0.2 collective-permute-start.6
  13.1 5.6 %collective-permute-done.2.ids = s32[1,128]{1,0:T(1,128)S(1)} collective-permute-done((s32[1,128]{1,0:T(1,128)S(1)}, s32[1,128]{1,0:T(1,128)S(1)}, u32[]{:S(2)}, u32[]{:S(2)}) %collective-permute-start.2) | collective-permute-done | bytes 544 | tf_op jit(solution)/shard_map/ppermute | solution.py:251
  18.7 0.0 collective-permute-done.1.rows
  18.7 0.1 collective-permute-start.3
  18.8 0.5 %collective-permute-start.7 = (s32[1,128]{1,0:T(1,128)S(1)}, s32[1,128]{1,0:T(1,128)S(1)}, u32[]{:S(2)}, u32[]{:S(2)}) collective-permute-start(s32[1,128]{1,0:T(1,128)S(1)} %bitcast.3), channel_id=1, source_target_pairs={{0,1},{1,0},{2,3},{3,2},{4,5},{5,4},{6,7},{7,6},{8,9},{9,8},{10,11... | collective-permute-start | bytes 1544 | tf_op jit(solution)/shard_map/ppermute | solution.py:251
  19.3 1.0 %collective-permute-done.7.own2_ids = s32[1,128]{1,0:T(1,128)S(1)} collective-permute-done((s32[1,128]{1,0:T(1,128)S(1)}, s32[1,128]{1,0:T(1,128)S(1)}, u32[]{:S(2)}, u32[]{:S(2)}) %collective-permute-start.7) | collective-permute-done | bytes 544 | tf_op jit(solution)/shard_map/ppermute | solution.py:251
  20.4 1.0 %collective-permute-start.8 = (bf16[72,1024]{1,0:T(8,128)(2,1)S(1)}, bf16[72,1024]{1,0:T(8,128)(2,1)S(1)}, u32[]{:S(2)}, u32[]{:S(2)}) collective-permute-start(bf16[72,1024]{1,0:T(8,128)(2,1)S(1)} %get-tuple-element.24), channel_id=1, source_target_pairs={{0,4},{1,5},{2,6},{3,7},{4,12},{5,13},{6,14},{7,15},{8,0},{9,1},{1... | collective-permute-start | bytes 442376 | tf_op jit(solution)/shard_map/ppermute | solution.py:251
  21.3 0.0 collective-permute-done.9.side
  21.3 0.0 collective-permute-start.11
  21.3 0.0 collective-permute-done.own2
  21.4 2.9 %collective-permute-start.10 = (bf16[64,1024]{1,0:T(8,128)(2,1)S(1)}, bf16[64,1024]{1,0:T(8,128)(2,1)S(1)}, u32[]{:S(2)}, u32[]{:S(2)}) collective-permute-start(bf16[64,1024]{1,0:T(8,128)(2,1)S(1)} %get-tuple-element.28), channel_id=1, source_target_pairs={{0,4},{1,5},{2,6},{3,7},{4,12},{5,13},{6,14},{7,15},{8,0},{9,1},{1... | collective-permute-start | bytes 393224 | tf_op jit(solution)/shard_map/ppermute | solution.py:251
  24.3 0.0 collective-permute-done.6.ring2
  24.3 0.0 collective-permute-done.3.col2
  24.3 1.5 %shard_map.30 = (bf16[128,1024]{1,0:T(8,128)(2,1)S(1)}, f32[128,1024]{1,0:T(8,128)S(1)}, f32[128,128]{1,0:T(8,128)S(1)}, bf16[136,1024]{1,0:T(8,128)(2,1)S(1)}) custom-call(bf16[128,1024]{1,0:T(8,128)(2,1)S(1)} %copy-done, bf16[128,1024]{1,0:T(8,128)(2,1)S(1)} %collective-permute-done.own2, bf16[136,1024]{1,0:T(8,128)(2,1)S(1)} %shard_map.28.col, ...), custom_call_target="tpu_custom_call" | custom-call | tf_op jit(solution)/shard_map/pallas_call | solution.py:231
  25.8 2.2 %collective-permute-done.8.fa = bf16[72,1024]{1,0:T(8,128)(2,1)S(1)} collective-permute-done((bf16[72,1024]{1,0:T(8,128)(2,1)S(1)}, bf16[72,1024]{1,0:T(8,128)(2,1)S(1)}, u32[]{:S(2)}, u32[]{:S(2)}) %collective-permute-start.8) | collective-permute-done | bytes 147488 | tf_op jit(solution)/shard_map/ppermute | solution.py:251
  28.0 0.0 collective-permute-start.12
  28.0 1.3 %collective-permute-start.13 = (bf16[72,1024]{1,0:T(8,128)(2,1)S(1)}, bf16[72,1024]{1,0:T(8,128)(2,1)S(1)}, u32[]{:S(2)}, u32[]{:S(2)}) collective-permute-start(bf16[72,1024]{1,0:T(8,128)(2,1)S(1)} %collective-permute-done.8.fa), channel_id=1, source_target_pairs={{0,2},{1,3},{2,0},{3,1},{4,6},{5,7},{6,4},{7,5},{8,10},{9,11},{10,... | collective-permute-start | bytes 442376 | tf_op jit(solution)/shard_map/ppermute | solution.py:251
  29.2 1.2 %collective-permute-start.18 = (bf16[136,1024]{1,0:T(8,128)(2,1)S(1)}, bf16[136,1024]{1,0:T(8,128)(2,1)S(1)}, u32[]{:S(2)}, u32[]{:S(2)}) collective-permute-start(bf16[136,1024]{1,0:T(8,128)(2,1)S(1)} %get-tuple-element.38), channel_id=1, source_target_pairs={{0,8},{1,9},{2,10},{3,11},{4,0},{5,1},{6,2},{7,3},{8,12},{9,13},{1... | collective-permute-start | bytes 835592 | tf_op jit(solution)/shard_map/ppermute | solution.py:251
  30.4 0.0 collective-permute-done.10.fb
  30.5 0.8 %collective-permute-start.15 = (bf16[64,1024]{1,0:T(8,128)(2,1)S(1)}, bf16[64,1024]{1,0:T(8,128)(2,1)S(1)}, u32[]{:S(2)}, u32[]{:S(2)}) collective-permute-start(bf16[64,1024]{1,0:T(8,128)(2,1)S(1)} %collective-permute-done.10.fb), channel_id=1, source_target_pairs={{0,2},{1,3},{2,0},{3,1},{4,6},{5,7},{6,4},{7,5},{8,10},{9,11},{10,... | collective-permute-start | bytes 393224 | tf_op jit(solution)/shard_map/ppermute | solution.py:251
  31.2 0.0 collective-permute-done.11.side2
  31.2 0.0 collective-permute-done.12.fa2
  31.2 0.9 %shard_map.31 = (f32[128,1024]{1,0:T(8,128)S(1)}, f32[128,128]{1,0:T(8,128)S(1)}) custom-call(bf16[128,1024]{1,0:T(8,128)(2,1)S(1)} %get-tuple-element.23.unit, s32[1,128]{1,0:T(1,128)S(1)} %bitcast.5, f32[128,1024]{1,0:T(8,128)S(1)} %get-tuple-element.26.sums, f32[128,128]{1,0:T(8,128)S(1)} %get-tuple-element.27.totals, ...), custom_call_target="tpu_custom_call" | custom-call | tf_op jit(solution)/shard_map/pallas_call | solution.py:231
  32.1 2.6 %collective-permute-done.13.sa = bf16[72,1024]{1,0:T(8,128)(2,1)S(1)} collective-permute-done((bf16[72,1024]{1,0:T(8,128)(2,1)S(1)}, bf16[72,1024]{1,0:T(8,128)(2,1)S(1)}, u32[]{:S(2)}, u32[]{:S(2)}) %collective-permute-start.13) | collective-permute-done | bytes 147488 | tf_op jit(solution)/shard_map/ppermute | solution.py:251
  34.7 0.0 collective-permute-start.16
  34.7 0.5 %collective-permute-start.14 = (bf16[64,1024]{1,0:T(8,128)(2,1)S(1)}, bf16[64,1024]{1,0:T(8,128)(2,1)S(1)}, u32[]{:S(2)}, u32[]{:S(2)}) collective-permute-start(bf16[64,1024]{1,0:T(8,128)(2,1)S(1)} %collective-permute-done.10.fb), channel_id=1, source_target_pairs={{0,1},{1,0},{2,3},{3,2},{4,5},{5,4},{6,7},{7,6},{8,9},{9,8},{10,11... | collective-permute-start | bytes 393224 | tf_op jit(solution)/shard_map/ppermute | solution.py:251
  35.2 1.8 %collective-permute-done.15.sb = bf16[64,1024]{1,0:T(8,128)(2,1)S(1)} collective-permute-done((bf16[64,1024]{1,0:T(8,128)(2,1)S(1)}, bf16[64,1024]{1,0:T(8,128)(2,1)S(1)}, u32[]{:S(2)}, u32[]{:S(2)}) %collective-permute-start.15) | collective-permute-done | bytes 131104 | tf_op jit(solution)/shard_map/ppermute | solution.py:251
  37.1 0.0 collective-permute-start.17
  37.1 0.0 collective-permute-done.14.fb2
  37.1 0.7 %shard_map.32 = (f32[128,1024]{1,0:T(8,128)S(1)}, f32[128,128]{1,0:T(8,128)S(1)}) custom-call(bf16[128,1024]{1,0:T(8,128)(2,1)S(1)} %get-tuple-element.23.unit, s32[1,128]{1,0:T(1,128)S(1)} %bitcast.6, f32[128,1024]{1,0:T(8,128)S(1)} %get-tuple-element.31.sums, f32[128,128]{1,0:T(8,128)S(1)} %get-tuple-element.33.totals, ...), custom_call_target="tpu_custom_call" | custom-call | tf_op jit(solution)/shard_map/pallas_call | solution.py:231
  37.8 0.6 %collective-permute-done.17.sb2 = bf16[64,1024]{1,0:T(8,128)(2,1)S(1)} collective-permute-done((bf16[64,1024]{1,0:T(8,128)(2,1)S(1)}, bf16[64,1024]{1,0:T(8,128)(2,1)S(1)}, u32[]{:S(2)}, u32[]{:S(2)}) %collective-permute-start.17) | collective-permute-done | bytes 131104 | tf_op jit(solution)/shard_map/ppermute | solution.py:251
  38.4 0.0 collective-permute-done.18.back
  38.4 0.0 collective-permute-done.16.sa2
  38.4 1.3 %shard_map.33 = bf16[128,1024]{1,0:T(8,128)(2,1)} custom-call(bf16[128,1024]{1,0:T(8,128)(2,1)S(1)} %get-tuple-element.23.unit, s32[1,128]{1,0:T(1,128)S(1)} %bitcast.7, f32[128,1024]{1,0:T(8,128)S(1)} %get-tuple-element.36.sums, f32[128,128]{1,0:T(8,128)S(1)} %get-tuple-element.37.totals, bf16[72,1024]{1,0:T(8,128)(2,1)S(1)} %collective-permute-done.16.sa2, ...), custom_call_target="tpu_custom_call" | custom-call | tf_op jit(solution)/shard_map/pallas_call | solution.py:231
  (2 shorter events, 0.1 us)
Async XLA Ops:
  0.0 12.4 %copy-start = (bf16[128,1024]{1,0:T(8,128)(2,1)S(1)}, bf16[128,1024]{1,0:T(8,128)(2,1)}, u32[]{:S(2)}) copy-start(bf16[128,1024]{1,0:T(8,128)(2,1)} %own.1) | copy-start | bytes 786436
  0.0 10.7 %collective-permute-start.4 = (bf16[128,1024]{1,0:T(8,128)(2,1)}, bf16[128,1024]{1,0:T(8,128)(2,1)S(1)}, u32[]{:S(2)}, u32[]{:S(2)}) collective-permute-start(bf16[128,1024]{1,0:T(8,128)(2,1)} %own.1), channel_id=1, source_target_pairs={{0,4},{1,5},{2,6},{3,7},{4,12},{5,13},{6,14},{7,15},{8,0},{9,1},{1... | collective-permute-start | bytes 786440 | tf_op jit(solution)/shard_map/ppermute | solution.py:251
  3.1 15.7 %collective-permute-start.1 = (bf16[128,1024]{1,0:T(8,128)(2,1)}, bf16[128,1024]{1,0:T(8,128)(2,1)S(1)}, u32[]{:S(2)}, u32[]{:S(2)}) collective-permute-start(bf16[128,1024]{1,0:T(8,128)(2,1)} %own.1), channel_id=1, source_target_pairs={{0,2},{1,3},{2,0},{3,1},{4,6},{5,7},{6,4},{7,5},{8,10},{9,11},{10,... | collective-permute-start | bytes 786440 | tf_op jit(solution)/shard_map/ppermute | solution.py:251
  4.6 6.2 %collective-permute-start.5 = (s32[1,128]{1,0:T(1,128)}, s32[1,128]{1,0:T(1,128)S(1)}, u32[]{:S(2)}, u32[]{:S(2)}) collective-permute-start(s32[1,128]{1,0:T(1,128)} %bitcast.1), channel_id=1, source_target_pairs={{0,4},{1,5},{2,6},{3,7},{4,12},{5,13},{6,14},{7,15},{8,0},{9,1},{1... | collective-permute-start | bytes 1544 | tf_op jit(solution)/shard_map/ppermute | solution.py:251
  10.8 1.6 %copy-start.1 = (s32[128]{0:T(128)S(1)}, s32[128]{0:T(128)}, u32[]{:S(2)}) copy-start(s32[128]{0:T(128)} %param.4) | copy-start | bytes 1540
  10.8 10.5 %collective-permute-start.9 = (bf16[136,1024]{1,0:T(8,128)(2,1)S(1)}, bf16[136,1024]{1,0:T(8,128)(2,1)S(1)}, u32[]{:S(2)}, u32[]{:S(2)}) collective-permute-start(bf16[136,1024]{1,0:T(8,128)(2,1)S(1)} %get-tuple-element.22.ring), channel_id=1, source_target_pairs={{0,2},{1,3},{2,0},{3,1},{4,6},{5,7},{6,4},{7,5},{8,10},{9,11},{10,... | collective-permute-start | bytes 835592 | tf_op jit(solution)/shard_map/ppermute | solution.py:251
  12.4 9.0 %collective-permute-start = (bf16[128,1024]{1,0:T(8,128)(2,1)S(1)}, bf16[128,1024]{1,0:T(8,128)(2,1)S(1)}, u32[]{:S(2)}, u32[]{:S(2)}) collective-permute-start(bf16[128,1024]{1,0:T(8,128)(2,1)S(1)} %copy-done), channel_id=1, source_target_pairs={{0,1},{1,0},{2,3},{3,2},{4,5},{5,4},{6,7},{7,6},{8,9},{9,8},{10,11... | collective-permute-start | bytes 786440 | tf_op jit(solution)/shard_map/ppermute | solution.py:251
  12.4 6.3 %collective-permute-start.2 = (s32[1,128]{1,0:T(1,128)S(1)}, s32[1,128]{1,0:T(1,128)S(1)}, u32[]{:S(2)}, u32[]{:S(2)}) collective-permute-start(s32[1,128]{1,0:T(1,128)S(1)} %bitcast.2), channel_id=1, source_target_pairs={{0,2},{1,3},{2,0},{3,1},{4,6},{5,7},{6,4},{7,5},{8,10},{9,11},{10,... | collective-permute-start | bytes 1544 | tf_op jit(solution)/shard_map/ppermute | solution.py:251
  13.0 11.3 %collective-permute-start.6 = (bf16[136,1024]{1,0:T(8,128)(2,1)S(1)}, bf16[136,1024]{1,0:T(8,128)(2,1)S(1)}, u32[]{:S(2)}, u32[]{:S(2)}) collective-permute-start(bf16[136,1024]{1,0:T(8,128)(2,1)S(1)} %get-tuple-element.22.ring), channel_id=1, source_target_pairs={{0,1},{1,0},{2,3},{3,2},{4,5},{5,4},{6,7},{7,6},{8,9},{9,8},{10,11... | collective-permute-start | bytes 835592 | tf_op jit(solution)/shard_map/ppermute | solution.py:251
  18.7 5.6 %collective-permute-start.3 = (bf16[136,1024]{1,0:T(8,128)(2,1)S(1)}, bf16[136,1024]{1,0:T(8,128)(2,1)S(1)}, u32[]{:S(2)}, u32[]{:S(2)}) collective-permute-start(bf16[136,1024]{1,0:T(8,128)(2,1)S(1)} %shard_map.28.col), channel_id=1, source_target_pairs={{0,1},{1,0},{2,3},{3,2},{4,5},{5,4},{6,7},{7,6},{8,9},{9,8},{10,11... | collective-permute-start | bytes 835592 | tf_op jit(solution)/shard_map/ppermute | solution.py:251
  18.8 1.5 %collective-permute-start.7 = (s32[1,128]{1,0:T(1,128)S(1)}, s32[1,128]{1,0:T(1,128)S(1)}, u32[]{:S(2)}, u32[]{:S(2)}) collective-permute-start(s32[1,128]{1,0:T(1,128)S(1)} %bitcast.3), channel_id=1, source_target_pairs={{0,1},{1,0},{2,3},{3,2},{4,5},{5,4},{6,7},{7,6},{8,9},{9,8},{10,11... | collective-permute-start | bytes 1544 | tf_op jit(solution)/shard_map/ppermute | solution.py:251
  20.4 7.6 %collective-permute-start.8 = (bf16[72,1024]{1,0:T(8,128)(2,1)S(1)}, bf16[72,1024]{1,0:T(8,128)(2,1)S(1)}, u32[]{:S(2)}, u32[]{:S(2)}) collective-permute-start(bf16[72,1024]{1,0:T(8,128)(2,1)S(1)} %get-tuple-element.24), channel_id=1, source_target_pairs={{0,4},{1,5},{2,6},{3,7},{4,12},{5,13},{6,14},{7,15},{8,0},{9,1},{1... | collective-permute-start | bytes 442376 | tf_op jit(solution)/shard_map/ppermute | solution.py:251
  21.3 9.9 %collective-permute-start.11 = (bf16[136,1024]{1,0:T(8,128)(2,1)S(1)}, bf16[136,1024]{1,0:T(8,128)(2,1)S(1)}, u32[]{:S(2)}, u32[]{:S(2)}) collective-permute-start(bf16[136,1024]{1,0:T(8,128)(2,1)S(1)} %collective-permute-done.9.side), channel_id=1, source_target_pairs={{0,1},{1,0},{2,3},{3,2},{4,5},{5,4},{6,7},{7,6},{8,9},{9,8},{10,11... | collective-permute-start | bytes 835592 | tf_op jit(solution)/shard_map/ppermute | solution.py:251
  21.4 9.1 %collective-permute-start.10 = (bf16[64,1024]{1,0:T(8,128)(2,1)S(1)}, bf16[64,1024]{1,0:T(8,128)(2,1)S(1)}, u32[]{:S(2)}, u32[]{:S(2)}) collective-permute-start(bf16[64,1024]{1,0:T(8,128)(2,1)S(1)} %get-tuple-element.28), channel_id=1, source_target_pairs={{0,4},{1,5},{2,6},{3,7},{4,12},{5,13},{6,14},{7,15},{8,0},{9,1},{1... | collective-permute-start | bytes 393224 | tf_op jit(solution)/shard_map/ppermute | solution.py:251
  28.0 3.2 %collective-permute-start.12 = (bf16[72,1024]{1,0:T(8,128)(2,1)S(1)}, bf16[72,1024]{1,0:T(8,128)(2,1)S(1)}, u32[]{:S(2)}, u32[]{:S(2)}) collective-permute-start(bf16[72,1024]{1,0:T(8,128)(2,1)S(1)} %collective-permute-done.8.fa), channel_id=1, source_target_pairs={{0,1},{1,0},{2,3},{3,2},{4,5},{5,4},{6,7},{7,6},{8,9},{9,8},{10,11... | collective-permute-start | bytes 442376 | tf_op jit(solution)/shard_map/ppermute | solution.py:251
  28.0 6.7 %collective-permute-start.13 = (bf16[72,1024]{1,0:T(8,128)(2,1)S(1)}, bf16[72,1024]{1,0:T(8,128)(2,1)S(1)}, u32[]{:S(2)}, u32[]{:S(2)}) collective-permute-start(bf16[72,1024]{1,0:T(8,128)(2,1)S(1)} %collective-permute-done.8.fa), channel_id=1, source_target_pairs={{0,2},{1,3},{2,0},{3,1},{4,6},{5,7},{6,4},{7,5},{8,10},{9,11},{10,... | collective-permute-start | bytes 442376 | tf_op jit(solution)/shard_map/ppermute | solution.py:251
  29.2 9.2 %collective-permute-start.18 = (bf16[136,1024]{1,0:T(8,128)(2,1)S(1)}, bf16[136,1024]{1,0:T(8,128)(2,1)S(1)}, u32[]{:S(2)}, u32[]{:S(2)}) collective-permute-start(bf16[136,1024]{1,0:T(8,128)(2,1)S(1)} %get-tuple-element.38), channel_id=1, source_target_pairs={{0,8},{1,9},{2,10},{3,11},{4,0},{5,1},{6,2},{7,3},{8,12},{9,13},{1... | collective-permute-start | bytes 835592 | tf_op jit(solution)/shard_map/ppermute | solution.py:251
  30.5 6.6 %collective-permute-start.15 = (bf16[64,1024]{1,0:T(8,128)(2,1)S(1)}, bf16[64,1024]{1,0:T(8,128)(2,1)S(1)}, u32[]{:S(2)}, u32[]{:S(2)}) collective-permute-start(bf16[64,1024]{1,0:T(8,128)(2,1)S(1)} %collective-permute-done.10.fb), channel_id=1, source_target_pairs={{0,2},{1,3},{2,0},{3,1},{4,6},{5,7},{6,4},{7,5},{8,10},{9,11},{10,... | collective-permute-start | bytes 393224 | tf_op jit(solution)/shard_map/ppermute | solution.py:251
  34.7 3.7 %collective-permute-start.16 = (bf16[72,1024]{1,0:T(8,128)(2,1)S(1)}, bf16[72,1024]{1,0:T(8,128)(2,1)S(1)}, u32[]{:S(2)}, u32[]{:S(2)}) collective-permute-start(bf16[72,1024]{1,0:T(8,128)(2,1)S(1)} %collective-permute-done.13.sa), channel_id=1, source_target_pairs={{0,1},{1,0},{2,3},{3,2},{4,5},{5,4},{6,7},{7,6},{8,9},{9,8},{10,11... | collective-permute-start | bytes 442376 | tf_op jit(solution)/shard_map/ppermute | solution.py:251
  34.7 2.4 %collective-permute-start.14 = (bf16[64,1024]{1,0:T(8,128)(2,1)S(1)}, bf16[64,1024]{1,0:T(8,128)(2,1)S(1)}, u32[]{:S(2)}, u32[]{:S(2)}) collective-permute-start(bf16[64,1024]{1,0:T(8,128)(2,1)S(1)} %collective-permute-done.10.fb), channel_id=1, source_target_pairs={{0,1},{1,0},{2,3},{3,2},{4,5},{5,4},{6,7},{7,6},{8,9},{9,8},{10,11... | collective-permute-start | bytes 393224 | tf_op jit(solution)/shard_map/ppermute | solution.py:251
  37.1 1.3 %collective-permute-start.17 = (bf16[64,1024]{1,0:T(8,128)(2,1)S(1)}, bf16[64,1024]{1,0:T(8,128)(2,1)S(1)}, u32[]{:S(2)}, u32[]{:S(2)}) collective-permute-start(bf16[64,1024]{1,0:T(8,128)(2,1)S(1)} %collective-permute-done.15.sb), channel_id=1, source_target_pairs={{0,1},{1,0},{2,3},{3,2},{4,5},{5,4},{6,7},{7,6},{8,9},{9,8},{10,11... | collective-permute-start | bytes 393224 | tf_op jit(solution)/shard_map/ppermute | solution.py:251

commit v3 on v2

--- a/solution.py
+++ b/solution.py
@@ -137,6 +137,17 @@
     store_row(out, n, n, jnp.broadcast_to(ids[...].astype(jnp.float32), (pad, n)))
 
 
+def load_body(rows, ids, near_rows, near_ids, sems):
+    copies = [
+        pltpu.make_async_copy(rows, near_rows, sems.at[0]),
+        pltpu.make_async_copy(ids, near_ids, sems.at[1]),
+    ]
+    for copy in copies:
+        copy.start()
+    for copy in copies:
+        copy.wait()
+
+
 def split_body(rows, ids, out, first, second):
     n = rows.shape[0]
     half = n // 2
@@ -148,30 +159,38 @@
     second[...] = rows[half:, :]
 
 
-def early_body(own, own2, col, col2, ring, ring2, own_ids, own2_ids, unit, sums, totals, back):
+def reply_body(own, own2, col, col2, ring, own_ids, own2_ids, units, back):
+    n = own.shape[0]
+    blocks = (col, col2, ring)
+    rows = [own[...], own2[...]] + [ref[:n, :] for ref in blocks]
+    ids = [ref[...].astype(jnp.float32) for ref in (own_ids, own2_ids)]
+    ids += [load_row(ref, n) for ref in blocks]
+    parts = [normalize(r) for r in rows]
+    weight, total = weights(parts[4], as_column(ids[4]), cat(parts[:4]), cat(ids[:4], 1))
+    numer = weighted(weight, cat(rows[:4]))
+    back[:n, :] = numer.astype(jnp.bfloat16)
+    store_row(back, n, n, as_rows(total))
+    for k, part in enumerate(parts):
+        units[k * n : (k + 1) * n, :] = part
+
+
+def rest_body(own, own2, col, col2, ring, ring2, own_ids, own2_ids, units, sums, totals):
     n = own.shape[0]
     blocks = (col, col2, ring, ring2)
     rows = [own[...], own2[...]] + [ref[:n, :] for ref in blocks]
     ids = [ref[...].astype(jnp.float32) for ref in (own_ids, own2_ids)]
     ids += [load_row(ref, n) for ref in blocks]
-    units = [normalize(r) for r in rows]
-    of_own, of_ring = as_column(ids[0]), as_column(ids[4])
     weight, total = weights(
-        cat([units[0], units[4]]), cat([of_own, of_ring]), cat(units[:4]), cat(ids[:4], 1)
-    )
-    numer = weighted(weight, cat(rows[:4]))
-    back[:n, :] = numer[n:].astype(jnp.bfloat16)
-    store_row(back, n, n, as_rows(total[n:]))
-    weight2, total2 = weights(units[0], of_own, cat(units[4:]), cat(ids[4:], 1))
-    unit[...] = units[0]
-    sums[...] = numer[:n] + weighted(weight2, cat(rows[4:]))
-    totals[...] = jnp.broadcast_to(total[:n] + total2, (n, n))
+        units[:n, :], as_column(ids[0]), cat([units[...], normalize(rows[5])]), cat(ids, 1)
+    )
+    sums[...] = weighted(weight, cat(rows))
+    totals[...] = jnp.broadcast_to(total, totals.shape)
 
 
 def key_sums(unit, ids, keys):
     rows = cat([row for row, _ in keys])
     weight, total = weights(
-        unit[...], as_column(ids[...].astype(jnp.float32)), cat([normalize(row) for row, _ in keys]),
+        unit[: ids.shape[1], :], as_column(ids[...].astype(jnp.float32)), cat([normalize(row) for row, _ in keys]),
         cat([row for _, row in keys], 1),
     )
     return weighted(weight, rows), total
@@ -196,20 +215,26 @@
 
 
 def mid_body(unit, ids, sums, totals, side, side2, fa, fa2, new_sums, new_totals):
-    n = unit.shape[0]
+    n = ids.shape[1]
     keys = [keys_of(side, n), keys_of(side2, n), first_of(fa, n), first_of(fa2, n)]
     add_to(sums, totals, new_sums, new_totals, unit, ids, keys)
 
 
-def late_body(unit, ids, sums, totals, fa, fa2, fb, fb2, sa, sb, new_sums, new_totals):
-    n = unit.shape[0]
-    keys = [second_of(fb, fa, n), second_of(fb2, fa2, n), first_of(sa, n), second_of(sb, sa, n)]
+def late_body(unit, ids, sums, totals, fa, fa2, fb, fb2, sa, new_sums, new_totals):
+    n = ids.shape[1]
+    keys = [second_of(fb, fa, n), second_of(fb2, fa2, n), first_of(sa, n)]
     add_to(sums, totals, new_sums, new_totals, unit, ids, keys)
 
 
+def last_body(unit, ids, sums, totals, sa, sa2, sb, new_sums, new_totals):
+    n = ids.shape[1]
+    keys = [first_of(sa2, n), second_of(sb, sa, n)]
+    add_to(sums, totals, new_sums, new_totals, unit, ids, keys)
+
+
 def finish_body(unit, ids, sums, totals, sa2, sb2, back, out, near_out, sems):
-    n = unit.shape[0]
-    numer, total = key_sums(unit, ids, [first_of(sa2, n), second_of(sb2, sa2, n)])
+    n = ids.shape[1]
+    numer, total = key_sums(unit, ids, [second_of(sb2, sa2, n)])
     scale = 1.0 / (total + totals[:, :1] + as_column(load_row(back, n)))
     step = n // 4
     copies = []
@@ -225,13 +250,12 @@
         copy.wait()
 
 
-def call(body, outs, *args, out_space=pltpu.VMEM, scratch=()):
-    vmem = pl.BlockSpec(memory_space=pltpu.VMEM)
+def call(body, outs, *args, in_space=pltpu.VMEM, out_space=pltpu.VMEM, scratch=()):
     kind = pltpu.VMEM if out_space is pltpu.VMEM else jax.ShapeDtypeStruct
     return pl.pallas_call(
         body,
         out_shape=[kind(shape, dtype) for shape, dtype in outs],
-        in_specs=[vmem] * len(args),
+        in_specs=[pl.BlockSpec(memory_space=in_space)] * len(args),
         out_specs=[pl.BlockSpec(memory_space=out_space)] * len(outs),
         scratch_shapes=scratch,
         compiler_params=pltpu.CompilerParams(vmem_limit_bytes=24 * 2**20),
@@ -264,6 +288,11 @@
     col_ids = send(ids, STAY, 1, 0)
     own2 = swap(own)
     own2_ids = swap(ids)
+    own, ids = call(
+        load_body, [((n, width), bf16), ((1, n), jnp.int32)], own, ids,
+        in_space=pl.ANY, scratch=[pltpu.SemaphoreType.DMA((2,))],
+    )
+    ring, own = lax.optimization_barrier((ring, own))
     packet1, packet2 = ((half + pad, width), bf16), ((half, width), bf16)
     ring, ra, rb = call(split_body, [packet, packet1, packet2], *near(ring, ring_ids))
     fa = send(ra, NEXT, 0, 0)
@@ -274,24 +303,25 @@
     col2 = swap(col)
 
     state = [((n, width), f32), ((n, n), f32)]
-    unit, sums, totals, back = call(
-        early_body,
-        [((n, width), bf16)] + state + [packet],
-        *near(own, own2, col, col2, ring, ring2, ids, own2_ids),
-    )
-    fa, sums = lax.optimization_barrier((fa, sums))
+    early = (own, own2, col, col2, ring)
+    unit, back = call(reply_body, [((5 * n, width), bf16), packet], *near(*early, ids, own2_ids))
+    fa, unit = lax.optimization_barrier((fa, unit))
     sa = send(fa, STAY, 1, 0)
     fa2 = swap(fa)
     back = send(back, BACK, 0, 0)
     sb = send(fb, STAY, 1, 0)
     fb2 = swap(fb)
     side2 = swap(side)
-    fb, side2 = lax.optimization_barrier((fb, side2))
+    fb, side, unit = lax.optimization_barrier((fb, side, unit))
+    sums, totals = call(rest_body, state, *near(*early, ring2, ids, own2_ids, unit))
+    side2, totals = lax.optimization_barrier((side2, totals))
     sums, totals = call(mid_body, state, *near(unit, ids, sums, totals, side, side2, fa, fa2))
     sa, totals = lax.optimization_barrier((sa, totals))
     sa2 = swap(sa)
+    sums, totals = call(late_body, state, *near(unit, ids, sums, totals, fa, fa2, fb, fb2, sa))
+    sb, totals = lax.optimization_barrier((sb, totals))
     sb2 = swap(sb)
-    sums, totals = call(late_body, state, *near(unit, ids, sums, totals, fa, fa2, fb, fb2, sa, sb))
+    sums, totals = call(last_body, state, *near(unit, ids, sums, totals, sa, sa2, sb))
     out = ((n, width), bf16)
     return call(
         finish_body, [out], *near(unit, ids, sums, totals, sa2, sb2, back),

time: 39.9 us -> 40.8 us (1.023)
  waiting for transfers between devices: 17.5 us -> 14.4 us
  local copies, waits for them, and re-layouts: 0.01 us -> 1.6 us
  Pallas kernels: 4.46 us -> 5.9 us
  starting transfers between devices: 17.7 us -> 18.7 us
    ppermute x19, waiting for transfers between devices: 17.5 us -> 14.4 us  [send(): return lax.ppermute(rows, 'dp', moves(layers, column, core))]
    unnamed x4, local copies, waits for them, and re-layouts: 0.01 us -> 1.6 us
    pallas_call x6 -> x9, Pallas kernels: 4.46 us -> 5.9 us  [call(): pl.pallas_call(body, out_shape=[kind(shape, dtype) for shape, dtype in ou...]
    ppermute x19, starting transfers between devices: 17.7 us -> 18.7 us  [send(): return lax.ppermute(rows, 'dp', moves(layers, column, core))]
  transfers between devices with their start and end apart: 19 -> 19, of which waited for: 7 -> 9; matrix products, arithmetic and copies ran while one was open for 0% -> 0% of each run, Pallas kernels for 8% -> 11%
where the time goes in v3:
time: 40.8 us; the launch traced here: 40.7 us
  starting transfers between devices  18.7 us (46%)
  waiting for transfers between devices  14.4 us (35%)
  Pallas kernels  5.9 us (14%)
  local copies, waits for them, and re-layouts  1.6 us (4%)
    ppermute x19, starting transfers between devices, send(): return lax.ppermute(rows, 'dp', moves(layers, column, core))  18.7 us
    ppermute x19, waiting for transfers between devices, send(): return lax.ppermute(rows, 'dp', moves(layers, column, core))  14.4 us
    pallas_call x9, Pallas kernels, call(): pl.pallas_call(body, out_shape=[kind(shape, dtype) for shape, dtype in ou...  5.9 us
    unnamed x4, local copies, waits for them, and re-layouts  1.6 us
  transfers between devices with their start and end apart: 19, of which 9 were waited for; matrix products, arithmetic and copies ran while one was open for 0% of the time, Pallas kernels for 11%

profile of v3, /device:TPU:0, one launch (start us, length us, event | category | flops | bytes accessed | tf_op | source)
XLA Modules:
  0.0 40.7 jit_solution(2818794465353407720)
XLA Ops:
  0.0 3.1 %collective-permute-start = (bf16[128,1024]{1,0:T(8,128)(2,1)}, bf16[128,1024]{1,0:T(8,128)(2,1)S(1)}, u32[]{:S(2)}, u32[]{:S(2)}) collective-permute-start(bf16[128,1024]{1,0:T(8,128)(2,1)} %rows.1), channel_id=1, source_target_pairs={{0,4},{1,5},{2,6},{3,7},{4,12},{5,13},{6,14},{7,15},{8,0},{9,1},{1... | collective-permute-start | bytes 786440 | tf_op jit(solution)/shard_map/ppermute | solution.py:275
  3.1 1.5 %collective-permute-start.6 = (bf16[128,1024]{1,0:T(8,128)(2,1)}, bf16[128,1024]{1,0:T(8,128)(2,1)S(1)}, u32[]{:S(2)}, u32[]{:S(2)}) collective-permute-start(bf16[128,1024]{1,0:T(8,128)(2,1)} %rows.1), channel_id=1, source_target_pairs={{0,2},{1,3},{2,0},{3,1},{4,6},{5,7},{6,4},{7,5},{8,10},{9,11},{10,... | collective-permute-start | bytes 786440 | tf_op jit(solution)/shard_map/ppermute | solution.py:275
  4.6 2.6 %collective-permute-start.1 = (s32[1,128]{1,0:T(1,128)}, s32[1,128]{1,0:T(1,128)S(1)}, u32[]{:S(2)}, u32[]{:S(2)}) collective-permute-start(s32[1,128]{1,0:T(1,128)} %bitcast.1), channel_id=1, source_target_pairs={{0,4},{1,5},{2,6},{3,7},{4,12},{5,13},{6,14},{7,15},{8,0},{9,1},{1... | collective-permute-start | bytes 1544 | tf_op jit(solution)/shard_map/ppermute | solution.py:275
  7.2 0.0 copy-start
  7.2 0.9 %copy-done = bf16[128,1024]{1,0:T(8,128)(2,1)S(1)} copy-done((bf16[128,1024]{1,0:T(8,128)(2,1)S(1)}, bf16[128,1024]{1,0:T(8,128)(2,1)}, u32[]{:S(2)}) %copy-start) | copy-done | bytes 262168
  8.1 0.0 copy-start.1
  8.1 0.7 %copy-done.1 = s32[128]{0:T(128)S(1)} copy-done((s32[128]{0:T(128)S(1)}, s32[128]{0:T(128)}, u32[]{:S(2)}) %copy-start.1) | copy-done | bytes 536
  8.8 1.8 %collective-permute-done.rows = bf16[128,1024]{1,0:T(8,128)(2,1)S(1)} collective-permute-done((bf16[128,1024]{1,0:T(8,128)(2,1)}, bf16[128,1024]{1,0:T(8,128)(2,1)S(1)}, u32[]{:S(2)}, u32[]{:S(2)}) %collective-permute-start) | collective-permute-done | bytes 262176 | tf_op jit(solution)/shard_map/ppermute | solution.py:275
  10.6 0.1 collective-permute-done.1.ids
  10.7 1.6 %collective-permute-start.3 = (bf16[136,1024]{1,0:T(8,128)(2,1)S(1)}, bf16[136,1024]{1,0:T(8,128)(2,1)S(1)}, u32[]{:S(2)}, u32[]{:S(2)}) collective-permute-start(bf16[136,1024]{1,0:T(8,128)(2,1)S(1)} %get-tuple-element.36.ring), channel_id=1, source_target_pairs={{0,2},{1,3},{2,0},{3,1},{4,6},{5,7},{6,4},{7,5},{8,10},{9,11},{10,... | collective-permute-start | bytes 835592 | tf_op jit(solution)/shard_map/ppermute | solution.py:275
  12.4 0.0 collective-permute-start.5
  12.4 0.5 %collective-permute-start.7 = (s32[1,128]{1,0:T(1,128)}, s32[1,128]{1,0:T(1,128)S(1)}, u32[]{:S(2)}, u32[]{:S(2)}) collective-permute-start(s32[1,128]{1,0:T(1,128)} %bitcast.2), channel_id=1, source_target_pairs={{0,2},{1,3},{2,0},{3,1},{4,6},{5,7},{6,4},{7,5},{8,10},{9,11},{10,... | collective-permute-start | bytes 1544 | tf_op jit(solution)/shard_map/ppermute | solution.py:275
  12.8 5.8 %collective-permute-done.7.ids = s32[1,128]{1,0:T(1,128)S(1)} collective-permute-done((s32[1,128]{1,0:T(1,128)}, s32[1,128]{1,0:T(1,128)S(1)}, u32[]{:S(2)}, u32[]{:S(2)}) %collective-permute-start.7) | collective-permute-done | bytes 544 | tf_op jit(solution)/shard_map/ppermute | solution.py:275
  18.6 0.0 collective-permute-done.6.rows
  18.6 0.1 collective-permute-start.8
  18.7 0.5 %collective-permute-start.10 = (bf16[136,1024]{1,0:T(8,128)(2,1)S(1)}, bf16[136,1024]{1,0:T(8,128)(2,1)S(1)}, u32[]{:S(2)}, u32[]{:S(2)}) collective-permute-start(bf16[136,1024]{1,0:T(8,128)(2,1)S(1)} %get-tuple-element.36.ring), channel_id=1, source_target_pairs={{0,1},{1,0},{2,3},{3,2},{4,5},{5,4},{6,7},{7,6},{8,9},{9,8},{10,11... | collective-permute-start | bytes 835592 | tf_op jit(solution)/shard_map/ppermute | solution.py:275
  19.2 0.0 collective-permute-done.3.side
  19.2 0.1 collective-permute-start.11
  19.3 0.4 %collective-permute-start.9 = (s32[1,128]{1,0:T(1,128)}, s32[1,128]{1,0:T(1,128)S(1)}, u32[]{:S(2)}, u32[]{:S(2)}) collective-permute-start(s32[1,128]{1,0:T(1,128)} %bitcast.3), channel_id=1, source_target_pairs={{0,1},{1,0},{2,3},{3,2},{4,5},{5,4},{6,7},{7,6},{8,9},{9,8},{10,11... | collective-permute-start | bytes 1544 | tf_op jit(solution)/shard_map/ppermute | solution.py:275
  19.7 1.3 %collective-permute-done.9.own2_ids = s32[1,128]{1,0:T(1,128)S(1)} collective-permute-done((s32[1,128]{1,0:T(1,128)}, s32[1,128]{1,0:T(1,128)S(1)}, u32[]{:S(2)}, u32[]{:S(2)}) %collective-permute-start.9) | collective-permute-done | bytes 544 | tf_op jit(solution)/shard_map/ppermute | solution.py:275
  21.1 1.1 %collective-permute-start.4 = (bf16[72,1024]{1,0:T(8,128)(2,1)S(1)}, bf16[72,1024]{1,0:T(8,128)(2,1)S(1)}, u32[]{:S(2)}, u32[]{:S(2)}) collective-permute-start(bf16[72,1024]{1,0:T(8,128)(2,1)S(1)} %get-tuple-element.37), channel_id=1, source_target_pairs={{0,4},{1,5},{2,6},{3,7},{4,12},{5,13},{6,14},{7,15},{8,0},{9,1},{1... | collective-permute-start | bytes 442376 | tf_op jit(solution)/shard_map/ppermute | solution.py:275
  22.1 0.0 collective-permute-done.5.own2
  22.1 2.9 %collective-permute-start.2 = (bf16[64,1024]{1,0:T(8,128)(2,1)S(1)}, bf16[64,1024]{1,0:T(8,128)(2,1)S(1)}, u32[]{:S(2)}, u32[]{:S(2)}) collective-permute-start(bf16[64,1024]{1,0:T(8,128)(2,1)S(1)} %get-tuple-element.35), channel_id=1, source_target_pairs={{0,4},{1,5},{2,6},{3,7},{4,12},{5,13},{6,14},{7,15},{8,0},{9,1},{1... | collective-permute-start | bytes 393224 | tf_op jit(solution)/shard_map/ppermute | solution.py:275
  25.0 0.0 collective-permute-done.8.col2
  25.0 1.1 %shard_map.31 = (bf16[640,1024]{1,0:T(8,128)(2,1)S(1)}, bf16[136,1024]{1,0:T(8,128)(2,1)S(1)}) custom-call(bf16[128,1024]{1,0:T(8,128)(2,1)S(1)} %get-tuple-element.38.own, bf16[128,1024]{1,0:T(8,128)(2,1)S(1)} %collective-permute-done.5.own2, bf16[136,1024]{1,0:T(8,128)(2,1)S(1)} %shard_map.30.col, bf16[136,1024]{1,0:T(8,128)(2,1)S(1)} %collective-permute-done.8.col2, ...), custom_call_target="tpu_custom_call" | custom-call | tf_op jit(solution)/shard_map/pallas_call | solution.py:255
  26.1 2.6 %collective-permute-done.4.fa = bf16[72,1024]{1,0:T(8,128)(2,1)S(1)} collective-permute-done((bf16[72,1024]{1,0:T(8,128)(2,1)S(1)}, bf16[72,1024]{1,0:T(8,128)(2,1)S(1)}, u32[]{:S(2)}, u32[]{:S(2)}) %collective-permute-start.4) | collective-permute-done | bytes 147488 | tf_op jit(solution)/shard_map/ppermute | solution.py:275
  28.7 0.0 collective-permute-start.12
  28.7 1.3 %collective-permute-start.13 = (bf16[72,1024]{1,0:T(8,128)(2,1)S(1)}, bf16[72,1024]{1,0:T(8,128)(2,1)S(1)}, u32[]{:S(2)}, u32[]{:S(2)}) collective-permute-start(bf16[72,1024]{1,0:T(8,128)(2,1)S(1)} %collective-permute-done.4.fa), channel_id=1, source_target_pairs={{0,2},{1,3},{2,0},{3,1},{4,6},{5,7},{6,4},{7,5},{8,10},{9,11},{10,... | collective-permute-start | bytes 442376 | tf_op jit(solution)/shard_map/ppermute | solution.py:275
  30.0 0.7 %collective-permute-done.2.fb = bf16[64,1024]{1,0:T(8,128)(2,1)S(1)} collective-permute-done((bf16[64,1024]{1,0:T(8,128)(2,1)S(1)}, bf16[64,1024]{1,0:T(8,128)(2,1)S(1)}, u32[]{:S(2)}, u32[]{:S(2)}) %collective-permute-start.2) | collective-permute-done | bytes 131104 | tf_op jit(solution)/shard_map/ppermute | solution.py:275
  30.7 1.3 %collective-permute-start.18 = (bf16[136,1024]{1,0:T(8,128)(2,1)S(1)}, bf16[136,1024]{1,0:T(8,128)(2,1)S(1)}, u32[]{:S(2)}, u32[]{:S(2)}) collective-permute-start(bf16[136,1024]{1,0:T(8,128)(2,1)S(1)} %get-tuple-element.60), channel_id=1, source_target_pairs={{0,8},{1,9},{2,10},{3,11},{4,0},{5,1},{6,2},{7,3},{8,12},{9,13},{1... | collective-permute-start | bytes 835592 | tf_op jit(solution)/shard_map/ppermute | solution.py:275
  32.0 0.0 collective-permute-done.10.ring2
  32.0 0.0 collective-permute-start.14
  32.0 0.0 collective-permute-done.11.side2
  32.0 1.6 %collective-permute-start.15 = (bf16[64,1024]{1,0:T(8,128)(2,1)S(1)}, bf16[64,1024]{1,0:T(8,128)(2,1)S(1)}, u32[]{:S(2)}, u32[]{:S(2)}) collective-permute-start(bf16[64,1024]{1,0:T(8,128)(2,1)S(1)} %collective-permute-done.2.fb), channel_id=1, source_target_pairs={{0,2},{1,3},{2,0},{3,1},{4,6},{5,7},{6,4},{7,5},{8,10},{9,11},{10,... | collective-permute-start | bytes 393224 | tf_op jit(solution)/shard_map/ppermute | solution.py:275
  33.6 1.2 %shard_map.32 = (f32[128,1024]{1,0:T(8,128)S(1)}, f32[128,128]{1,0:T(8,128)S(1)}) custom-call(bf16[128,1024]{1,0:T(8,128)(2,1)S(1)} %get-tuple-element.38.own, bf16[128,1024]{1,0:T(8,128)(2,1)S(1)} %collective-permute-done.5.own2, bf16[136,1024]{1,0:T(8,128)(2,1)S(1)} %shard_map.30.col, bf16[136,1024]{1,0:T(8,128)(2,1)S(1)} %collective-permute-done.8.col2, ...), custom_call_target="tpu_custom_call" | custom-call | tf_op jit(solution)/shard_map/pallas_call | solution.py:255
  34.8 0.0 collective-permute-done.12.fa2
  34.8 0.9 %shard_map.33 = (f32[128,1024]{1,0:T(8,128)S(1)}, f32[128,128]{1,0:T(8,128)S(1)}) custom-call(bf16[640,1024]{1,0:T(8,128)(2,1)S(1)} %get-tuple-element.42.units.unit, s32[1,128]{1,0:T(1,128)S(1)} %get-tuple-element.39.own_ids.ids, f32[128,1024]{1,0:T(8,128)S(1)} %get-tuple-element.43.sums, f32[128,128]{1,0:T(8,128)S(1)} %get-tuple-element.45.totals, ...), custom_call_target="tpu_custom_call" | custom-call | tf_op jit(solution)/shard_map/pallas_call | solution.py:255
  35.7 0.0 collective-permute-done.13.sa
  35.7 0.2 collective-permute-start.16
  35.9 0.0 collective-permute-done.14.fb2
  35.9 0.7 %shard_map.34 = (f32[128,1024]{1,0:T(8,128)S(1)}, f32[128,128]{1,0:T(8,128)S(1)}) custom-call(bf16[640,1024]{1,0:T(8,128)(2,1)S(1)} %get-tuple-element.42.units.unit, s32[1,128]{1,0:T(1,128)S(1)} %get-tuple-element.39.own_ids.ids, f32[128,1024]{1,0:T(8,128)S(1)} %get-tuple-element.49.sums, f32[128,128]{1,0:T(8,128)S(1)} %get-tuple-element.51.totals, ...), custom_call_target="tpu_custom_call" | custom-call | tf_op jit(solution)/shard_map/pallas_call | solution.py:255
  36.6 1.3 %collective-permute-done.15.sb = bf16[64,1024]{1,0:T(8,128)(2,1)S(1)} collective-permute-done((bf16[64,1024]{1,0:T(8,128)(2,1)S(1)}, bf16[64,1024]{1,0:T(8,128)(2,1)S(1)}, u32[]{:S(2)}, u32[]{:S(2)}) %collective-permute-start.15) | collective-permute-done | bytes 131104 | tf_op jit(solution)/shard_map/ppermute | solution.py:275
  37.9 0.0 collective-permute-start.17
  37.9 0.0 collective-permute-done.16.sa2
  37.9 0.5 %shard_map.35 = (f32[128,1024]{1,0:T(8,128)S(1)}, f32[128,128]{1,0:T(8,128)S(1)}) custom-call(bf16[640,1024]{1,0:T(8,128)(2,1)S(1)} %get-tuple-element.42.units.unit, s32[1,128]{1,0:T(1,128)S(1)} %get-tuple-element.39.own_ids.ids, f32[128,1024]{1,0:T(8,128)S(1)} %get-tuple-element.54.sums, f32[128,128]{1,0:T(8,128)S(1)} %get-tuple-element.56.totals, ...), custom_call_target="tpu_custom_call" | custom-call | tf_op jit(solution)/shard_map/pallas_call | solution.py:255
  38.4 0.4 collective-permute-done.18.back
  38.8 0.5 %collective-permute-done.17.sb2 = bf16[64,1024]{1,0:T(8,128)(2,1)S(1)} collective-permute-done((bf16[64,1024]{1,0:T(8,128)(2,1)S(1)}, bf16[64,1024]{1,0:T(8,128)(2,1)S(1)}, u32[]{:S(2)}, u32[]{:S(2)}) %collective-permute-start.17) | collective-permute-done | bytes 131104 | tf_op jit(solution)/shard_map/ppermute | solution.py:275
  39.2 1.4 %shard_map.36 = bf16[128,1024]{1,0:T(8,128)(2,1)} custom-call(bf16[640,1024]{1,0:T(8,128)(2,1)S(1)} %get-tuple-element.42.units.unit, s32[1,128]{1,0:T(1,128)S(1)} %get-tuple-element.39.own_ids.ids, f32[128,1024]{1,0:T(8,128)S(1)} %get-tuple-element.58.sums, f32[128,128]{1,0:T(8,128)S(1)} %get-tuple-element.59.totals, ...), custom_call_target="tpu_custom_call" | custom-call | tf_op jit(solution)/shard_map/pallas_call | solution.py:255
  (3 shorter events, 0.1 us)
Async XLA Ops:
  0.0 10.6 %collective-permute-start = (bf16[128,1024]{1,0:T(8,128)(2,1)}, bf16[128,1024]{1,0:T(8,128)(2,1)S(1)}, u32[]{:S(2)}, u32[]{:S(2)}) collective-permute-start(bf16[128,1024]{1,0:T(8,128)(2,1)} %rows.1), channel_id=1, source_target_pairs={{0,4},{1,5},{2,6},{3,7},{4,12},{5,13},{6,14},{7,15},{8,0},{9,1},{1... | collective-permute-start | bytes 786440 | tf_op jit(solution)/shard_map/ppermute | solution.py:275
  3.1 15.6 %collective-permute-start.6 = (bf16[128,1024]{1,0:T(8,128)(2,1)}, bf16[128,1024]{1,0:T(8,128)(2,1)S(1)}, u32[]{:S(2)}, u32[]{:S(2)}) collective-permute-start(bf16[128,1024]{1,0:T(8,128)(2,1)} %rows.1), channel_id=1, source_target_pairs={{0,2},{1,3},{2,0},{3,1},{4,6},{5,7},{6,4},{7,5},{8,10},{9,11},{10,... | collective-permute-start | bytes 786440 | tf_op jit(solution)/shard_map/ppermute | solution.py:275
  4.6 6.1 %collective-permute-start.1 = (s32[1,128]{1,0:T(1,128)}, s32[1,128]{1,0:T(1,128)S(1)}, u32[]{:S(2)}, u32[]{:S(2)}) collective-permute-start(s32[1,128]{1,0:T(1,128)} %bitcast.1), channel_id=1, source_target_pairs={{0,4},{1,5},{2,6},{3,7},{4,12},{5,13},{6,14},{7,15},{8,0},{9,1},{1... | collective-permute-start | bytes 1544 | tf_op jit(solution)/shard_map/ppermute | solution.py:275
  7.2 0.9 %copy-start = (bf16[128,1024]{1,0:T(8,128)(2,1)S(1)}, bf16[128,1024]{1,0:T(8,128)(2,1)}, u32[]{:S(2)}) copy-start(bf16[128,1024]{1,0:T(8,128)(2,1)} %rows.1) | copy-start | bytes 786436
  8.1 0.7 %copy-start.1 = (s32[128]{0:T(128)S(1)}, s32[128]{0:T(128)}, u32[]{:S(2)}) copy-start(s32[128]{0:T(128)} %param.4) | copy-start | bytes 1540
  10.7 8.5 %collective-permute-start.3 = (bf16[136,1024]{1,0:T(8,128)(2,1)S(1)}, bf16[136,1024]{1,0:T(8,128)(2,1)S(1)}, u32[]{:S(2)}, u32[]{:S(2)}) collective-permute-start(bf16[136,1024]{1,0:T(8,128)(2,1)S(1)} %get-tuple-element.36.ring), channel_id=1, source_target_pairs={{0,2},{1,3},{2,0},{3,1},{4,6},{5,7},{6,4},{7,5},{8,10},{9,11},{10,... | collective-permute-start | bytes 835592 | tf_op jit(solution)/shard_map/ppermute | solution.py:275
  12.4 9.8 %collective-permute-start.5 = (bf16[128,1024]{1,0:T(8,128)(2,1)}, bf16[128,1024]{1,0:T(8,128)(2,1)S(1)}, u32[]{:S(2)}, u32[]{:S(2)}) collective-permute-start(bf16[128,1024]{1,0:T(8,128)(2,1)} %rows.1), channel_id=1, source_target_pairs={{0,1},{1,0},{2,3},{3,2},{4,5},{5,4},{6,7},{7,6},{8,9},{9,8},{10,11... | collective-permute-start | bytes 786440 | tf_op jit(solution)/shard_map/ppermute | solution.py:275
  12.4 6.3 %collective-permute-start.7 = (s32[1,128]{1,0:T(1,128)}, s32[1,128]{1,0:T(1,128)S(1)}, u32[]{:S(2)}, u32[]{:S(2)}) collective-permute-start(s32[1,128]{1,0:T(1,128)} %bitcast.2), channel_id=1, source_target_pairs={{0,2},{1,3},{2,0},{3,1},{4,6},{5,7},{6,4},{7,5},{8,10},{9,11},{10,... | collective-permute-start | bytes 1544 | tf_op jit(solution)/shard_map/ppermute | solution.py:275
  18.6 6.4 %collective-permute-start.8 = (bf16[136,1024]{1,0:T(8,128)(2,1)S(1)}, bf16[136,1024]{1,0:T(8,128)(2,1)S(1)}, u32[]{:S(2)}, u32[]{:S(2)}) collective-permute-start(bf16[136,1024]{1,0:T(8,128)(2,1)S(1)} %shard_map.30.col), channel_id=1, source_target_pairs={{0,1},{1,0},{2,3},{3,2},{4,5},{5,4},{6,7},{7,6},{8,9},{9,8},{10,11... | collective-permute-start | bytes 835592 | tf_op jit(solution)/shard_map/ppermute | solution.py:275
  18.7 13.2 %collective-permute-start.10 = (bf16[136,1024]{1,0:T(8,128)(2,1)S(1)}, bf16[136,1024]{1,0:T(8,128)(2,1)S(1)}, u32[]{:S(2)}, u32[]{:S(2)}) collective-permute-start(bf16[136,1024]{1,0:T(8,128)(2,1)S(1)} %get-tuple-element.36.ring), channel_id=1, source_target_pairs={{0,1},{1,0},{2,3},{3,2},{4,5},{5,4},{6,7},{7,6},{8,9},{9,8},{10,11... | collective-permute-start | bytes 835592 | tf_op jit(solution)/shard_map/ppermute | solution.py:275
  19.2 12.7 %collective-permute-start.11 = (bf16[136,1024]{1,0:T(8,128)(2,1)S(1)}, bf16[136,1024]{1,0:T(8,128)(2,1)S(1)}, u32[]{:S(2)}, u32[]{:S(2)}) collective-permute-start(bf16[136,1024]{1,0:T(8,128)(2,1)S(1)} %collective-permute-done.3.side), channel_id=1, source_target_pairs={{0,1},{1,0},{2,3},{3,2},{4,5},{5,4},{6,7},{7,6},{8,9},{9,8},{10,11... | collective-permute-start | bytes 835592 | tf_op jit(solution)/shard_map/ppermute | solution.py:275
  19.3 1.8 %collective-permute-start.9 = (s32[1,128]{1,0:T(1,128)}, s32[1,128]{1,0:T(1,128)S(1)}, u32[]{:S(2)}, u32[]{:S(2)}) collective-permute-start(s32[1,128]{1,0:T(1,128)} %bitcast.3), channel_id=1, source_target_pairs={{0,1},{1,0},{2,3},{3,2},{4,5},{5,4},{6,7},{7,6},{8,9},{9,8},{10,11... | collective-permute-start | bytes 1544 | tf_op jit(solution)/shard_map/ppermute | solution.py:275
  21.1 7.6 %collective-permute-start.4 = (bf16[72,1024]{1,0:T(8,128)(2,1)S(1)}, bf16[72,1024]{1,0:T(8,128)(2,1)S(1)}, u32[]{:S(2)}, u32[]{:S(2)}) collective-permute-start(bf16[72,1024]{1,0:T(8,128)(2,1)S(1)} %get-tuple-element.37), channel_id=1, source_target_pairs={{0,4},{1,5},{2,6},{3,7},{4,12},{5,13},{6,14},{7,15},{8,0},{9,1},{1... | collective-permute-start | bytes 442376 | tf_op jit(solution)/shard_map/ppermute | solution.py:275
  22.1 8.5 %collective-permute-start.2 = (bf16[64,1024]{1,0:T(8,128)(2,1)S(1)}, bf16[64,1024]{1,0:T(8,128)(2,1)S(1)}, u32[]{:S(2)}, u32[]{:S(2)}) collective-permute-start(bf16[64,1024]{1,0:T(8,128)(2,1)S(1)} %get-tuple-element.35), channel_id=1, source_target_pairs={{0,4},{1,5},{2,6},{3,7},{4,12},{5,13},{6,14},{7,15},{8,0},{9,1},{1... | collective-permute-start | bytes 393224 | tf_op jit(solution)/shard_map/ppermute | solution.py:275
  28.7 6.1 %collective-permute-start.12 = (bf16[72,1024]{1,0:T(8,128)(2,1)S(1)}, bf16[72,1024]{1,0:T(8,128)(2,1)S(1)}, u32[]{:S(2)}, u32[]{:S(2)}) collective-permute-start(bf16[72,1024]{1,0:T(8,128)(2,1)S(1)} %collective-permute-done.4.fa), channel_id=1, source_target_pairs={{0,1},{1,0},{2,3},{3,2},{4,5},{5,4},{6,7},{7,6},{8,9},{9,8},{10,11... | collective-permute-start | bytes 442376 | tf_op jit(solution)/shard_map/ppermute | solution.py:275
  28.7 7.0 %collective-permute-start.13 = (bf16[72,1024]{1,0:T(8,128)(2,1)S(1)}, bf16[72,1024]{1,0:T(8,128)(2,1)S(1)}, u32[]{:S(2)}, u32[]{:S(2)}) collective-permute-start(bf16[72,1024]{1,0:T(8,128)(2,1)S(1)} %collective-permute-done.4.fa), channel_id=1, source_target_pairs={{0,2},{1,3},{2,0},{3,1},{4,6},{5,7},{6,4},{7,5},{8,10},{9,11},{10,... | collective-permute-start | bytes 442376 | tf_op jit(solution)/shard_map/ppermute | solution.py:275
  30.7 8.1 %collective-permute-start.18 = (bf16[136,1024]{1,0:T(8,128)(2,1)S(1)}, bf16[136,1024]{1,0:T(8,128)(2,1)S(1)}, u32[]{:S(2)}, u32[]{:S(2)}) collective-permute-start(bf16[136,1024]{1,0:T(8,128)(2,1)S(1)} %get-tuple-element.60), channel_id=1, source_target_pairs={{0,8},{1,9},{2,10},{3,11},{4,0},{5,1},{6,2},{7,3},{8,12},{9,13},{1... | collective-permute-start | bytes 835592 | tf_op jit(solution)/shard_map/ppermute | solution.py:275
  32.0 3.9 %collective-permute-start.14 = (bf16[64,1024]{1,0:T(8,128)(2,1)S(1)}, bf16[64,1024]{1,0:T(8,128)(2,1)S(1)}, u32[]{:S(2)}, u32[]{:S(2)}) collective-permute-start(bf16[64,1024]{1,0:T(8,128)(2,1)S(1)} %collective-permute-done.2.fb), channel_id=1, source_target_pairs={{0,1},{1,0},{2,3},{3,2},{4,5},{5,4},{6,7},{7,6},{8,9},{9,8},{10,11... | collective-permute-start | bytes 393224 | tf_op jit(solution)/shard_map/ppermute | solution.py:275
  32.0 5.9 %collective-permute-start.15 = (bf16[64,1024]{1,0:T(8,128)(2,1)S(1)}, bf16[64,1024]{1,0:T(8,128)(2,1)S(1)}, u32[]{:S(2)}, u32[]{:S(2)}) collective-permute-start(bf16[64,1024]{1,0:T(8,128)(2,1)S(1)} %collective-permute-done.2.fb), channel_id=1, source_target_pairs={{0,2},{1,3},{2,0},{3,1},{4,6},{5,7},{6,4},{7,5},{8,10},{9,11},{10,... | collective-permute-start | bytes 393224 | tf_op jit(solution)/shard_map/ppermute | solution.py:275
  35.7 2.2 %collective-permute-start.16 = (bf16[72,1024]{1,0:T(8,128)(2,1)S(1)}, bf16[72,1024]{1,0:T(8,128)(2,1)S(1)}, u32[]{:S(2)}, u32[]{:S(2)}) collective-permute-start(bf16[72,1024]{1,0:T(8,128)(2,1)S(1)} %collective-permute-done.13.sa), channel_id=1, source_target_pairs={{0,1},{1,0},{2,3},{3,2},{4,5},{5,4},{6,7},{7,6},{8,9},{9,8},{10,11... | collective-permute-start | bytes 442376 | tf_op jit(solution)/shard_map/ppermute | solution.py:275
  37.9 1.3 %collective-permute-start.17 = (bf16[64,1024]{1,0:T(8,128)(2,1)S(1)}, bf16[64,1024]{1,0:T(8,128)(2,1)S(1)}, u32[]{:S(2)}, u32[]{:S(2)}) collective-permute-start(bf16[64,1024]{1,0:T(8,128)(2,1)S(1)} %collective-permute-done.15.sb), channel_id=1, source_target_pairs={{0,1},{1,0},{2,3},{3,2},{4,5},{5,4},{6,7},{7,6},{8,9},{9,8},{10,11... | collective-permute-start | bytes 393224 | tf_op jit(solution)/shard_map/ppermute | solution.py:275
